TPU v7x, 32 devices: a whole 2x2x4 slice. The times are simulated.
32 devices in a mesh: groups: 2 (over y), wide: 16 (over z, x, core).
Axes of the slice: x: 2, y: 2, z: 4, core: 2. Of those that a mesh axis runs over, the one named last changes fastest.
Arguments:
- fields: bfloat16 [32, 512], P(('groups', 'wide')), parts along dimension 0, may hold values from -6 to 6
- chol: bfloat16 [512, 1024, 1024], P(None, 'wide'), may hold values from -0.01171875 to 0.01171875
- orbitals: bfloat16 [32, 1024, 256], P(('groups', 'wide')), parts along dimension 0, may hold values from -6 to 6
- trial: bfloat16 [1024, 256], replicated, may hold values from -0.5 to 0.5
Outputs:
- new_orbitals: bfloat16 [32, 1024, 256], P(('groups', 'wide')), parts along dimension 0
- force_bias: float32 [32, 2, 512], P(('groups', 'wide')), parts along dimension 0
There are 2 independent parts, one for each index of `groups`. A program takes and returns all parts, laid end to end along the dimension named above; an argument that names none is the same for every part. Nothing has to cross between parts.
All inputs are finite; a program needn't handle non-finite values.
Results may differ from a plain program's by a relative error of at most 0.0075.
Values may be sent and summed in bfloat16 or wider, within the bound.
No kernel may reach another device: no remote copies, remote signals or barrier semaphores. Data moves between devices by JAX's collectives and lax.ppermute only.
A program may use at most 192 MiB of HBM per device.

v0:
```python
import jax
import jax.numpy as jnp
from jax import lax
from jax.sharding import PartitionSpec as P

TAYLOR = 4


def per_device(fields, chol, orbitals, trial):
    all_fields = lax.all_gather(fields, "wide", axis=0, tiled=True)
    vectors, rows, width = chol.shape
    chol_flat = chol.reshape(vectors, rows * width)
    generator = jnp.dot(all_fields, chol_flat, preferred_element_type=jnp.float32).astype(
        jnp.bfloat16
    )
    generator = generator.reshape(all_fields.shape[0], rows, width)
    owned = lax.all_to_all(generator, "wide", split_axis=0, concat_axis=1, tiled=True)
    nocc = orbitals.shape[2] // 2
    walk_local = orbitals.shape[0]
    gen_walker = owned[0]
    total = orbitals[0].astype(jnp.float32)
    operand = orbitals[0]
    for order in range(1, TAYLOR + 1):
        product = jnp.dot(gen_walker, operand, preferred_element_type=jnp.float32)
        term = jnp.concatenate([-product[:, nocc:], product[:, :nocc]], axis=1) / order
        total = total + term
        if order < TAYLOR:
            operand = term.astype(jnp.bfloat16)
    fresh_list = [total.astype(jnp.bfloat16)]
    new_orbitals = jnp.stack(fresh_list, axis=0)
    trial_real = trial[:, :nocc].T
    trial_imag = trial[:, nocc:].T
    mixer = jnp.concatenate(
        [
            jnp.concatenate([trial_real, -trial_imag], axis=1),
            jnp.concatenate([trial_imag, trial_real], axis=1),
        ],
        axis=0,
    )
    orbital_rows = lax.all_to_all(new_orbitals, "wide", split_axis=1, concat_axis=0, tiled=True)
    count = orbital_rows.shape[0]
    flat_rows = orbital_rows.reshape(count * rows, 2 * nocc)
    tile_green = jnp.dot(flat_rows, mixer, preferred_element_type=jnp.float32).astype(jnp.bfloat16)
    tile_green = tile_green.reshape(count, rows, 2 * width)
    all_walk = tile_green.shape[0]
    tile_green = (
        tile_green.reshape(all_walk, rows, 2, width)
        .transpose(0, 2, 1, 3)
        .reshape(all_walk * 2, rows * width)
    )
    partial_value = jnp.dot(tile_green, chol_flat.T, preferred_element_type=jnp.float32).reshape(
        all_walk, 2, vectors
    )
    summed = lax.psum(partial_value, "wide")
    force_bias = lax.dynamic_slice_in_dim(
        summed, lax.axis_index("wide") * walk_local, walk_local, 0
    )
    return (new_orbitals, force_bias)


def solution(mesh):
    in_specs = (
        P(("groups", "wide"), None),
        P(None, "wide", None),
        P(("groups", "wide"), None, None),
        P(),
    )
    out_specs = (P(("groups", "wide"), None, None), P(("groups", "wide"), None, None))
    return jax.shard_map(
        per_device, mesh=mesh, in_specs=in_specs, out_specs=out_specs, check_vma=False
    )
```

profile of v0, /device:TPU:0, one launch (start us, length us, event | category | flops | bytes accessed | tf_op | source)
XLA Modules:
  0.0 380.4 jit_solution(17390543338026890626)
XLA Ops:
  7.2 58.5 %copy.31 = bf16[64,8,64,1024]{3,1,2,0:T(8,128)(2,1)} copy(bf16[64,8,64,1024]{3,2,1,0:T(8,128)(2,1)} %bitcast.19) | data formatting | bytes 134217728
  65.7 23.2 %all-gather = bf16[16,1,512]{2,1,0:T(2,128)(2,1)S(1)} all-gather(bf16[1,1,512]{2,1,0:T(2,128)(2,1)S(1)} %bitcast.65), channel_id=1, replica_groups=mesh['groups'=2,'wide'=16] {'wide'}, dimensions={0}, use_global_device_ids=true | all-gather | bytes 17408 | tf_op jit(solution)/shard_map/all_gather | solution.py:10
  88.9 22.8 %convolution_convert_fusion = bf16[16,65536]{1,0:T(8,128)(2,1)S(1)} fusion(bf16[512,65536]{1,0:T(8,128)(2,1)} %bitcast.20, bf16[16,1,512]{2,1,0:T(2,128)(2,1)S(1)} %all-gather), kind=kOutput, calls=%fused_computation | convolution fusion | flops 1074790400 | bytes 69222400 | tf_op jit(solution)/shard_map/dot_general | solution.py:13
  111.7 2.5 copy.32
  114.2 4.0 %all-to-all-start = ((bf16[16,64,1024]{2,1,0:T(8,128)(2,1)}), bf16[16,64,1024]{2,1,0:T(8,128)(2,1)S(1)}, u32[]{:S(2)}, u32[]{:S(2)}) async-start(bf16[16,64,1024]{2,1,0:T(8,128)(2,1)} %bitcast.62), calls=%async_computation | async-start | bytes 4194304 | tf_op jit(solution)/shard_map/all_to_all | solution.py:17
  118.2 0.2 copy.22
  118.4 40.5 %all-to-all-done = bf16[16,64,1024]{2,1,0:T(8,128)(2,1)S(1)} async-done(((bf16[16,64,1024]{2,1,0:T(8,128)(2,1)}), bf16[16,64,1024]{2,1,0:T(8,128)(2,1)S(1)}, u32[]{:S(2)}, u32[]{:S(2)}) %all-to-all-start) | async-done | bytes 2097184 | tf_op jit(solution)/shard_map/all_to_all | solution.py:17
  158.9 0.8 fusion.34
  159.7 0.1 fusion.38
  159.9 0.7 fusion.28
  160.6 0.1 slice_negate_fusion.2
  160.8 0.7 fusion.25
  161.5 0.1 slice_negate_fusion.1
  161.7 0.7 fusion.23
  162.4 0.1 fusion.27
  162.5 0.6 fusion.13
  163.1 0.9 copy.23
  163.9 0.5 broadcast.24
  164.4 3.8 %reduce = bf16[1024,256]{1,0:T(8,128)(2,1)S(1)} reduce(bf16[1024,1,256]{2,1,0:T(2,128)(2,1)S(1)} %bitcast.63, bf16[]{:T(256)} %broadcast.24), dimensions={1}, to_apply=%bitcast.50.reduce_sub_computation | reduce | bytes 1048578
  168.3 0.9 reshape.121
  169.2 11.2 %all-to-all-start.1 = ((bf16[16,2,8192]{2,1,0:T(2,128)(2,1)}), bf16[16,2,8192]{2,1,0:T(2,128)(2,1)S(1)}, u32[]{:S(2)}, u32[]{:S(2)}) async-start(bf16[16,2,8192]{2,1,0:T(2,128)(2,1)} %reshape.121), calls=%async_computation.1 | async-start | bytes 1048576 | tf_op jit(solution)/shard_map/all_to_all | solution.py:40
  180.4 0.0 all-reduce.2.cloned.1.call-start
  180.5 14.1 %all-to-all-done.1 = bf16[16,2,8192]{2,1,0:T(2,128)(2,1)S(1)} async-done(((bf16[16,2,8192]{2,1,0:T(2,128)(2,1)}), bf16[16,2,8192]{2,1,0:T(2,128)(2,1)S(1)}, u32[]{:S(2)}, u32[]{:S(2)}) %all-to-all-start.1) | async-done | bytes 524320 | tf_op jit(solution)/shard_map/all_to_all | solution.py:40
  194.7 0.5 reshape.122
  195.2 3.3 convolution_convert_fusion.1
  198.5 7.8 %reshape_reshape.3 = bf16[16,64,2,1024]{3,2,1,0:T(2,128)(2,1)} reshape(bf16[1024,2048]{1,0:T(8,128)(2,1)} %convolution_convert_fusion.1) | data formatting | bytes 8388608 | tf_op jit(solution)/shard_map/reshape;reshape | solution.py:47
  206.2 80.0 %fusion.5 = f32[16,2,512]{2,0,1:T(8,128)} fusion(bf16[512,64,1024]{2,1,0:T(8,128)(2,1)} %param.5, bf16[16,64,2,1024]{3,2,1,0:T(2,128)(2,1)} %reshape_reshape.3), kind=kOutput, calls=%fused_computation.7 | convolution fusion | flops 2147483648 | bytes 71368704 | tf_op jit(solution)/shard_map/dot_general | solution.py:51
  286.2 0.0 all-reduce.2.cloned.1.call-update
  286.2 1.0 copy.26
  287.2 85.0 %all-reduce.2.cloned.1.call-done = f32[16,2,512]{2,0,1:T(8,128)} async-done(((f32[16,2,512]{2,0,1:T(8,128)}), f32[16,2,512]{2,0,1:T(8,128)}) %all-reduce.2.cloned.1.call-update) | async-done | bytes 65552 | tf_op jit(solution)/shard_map/psum | solution.py:54
  372.2 0.8 constant_dynamic-slice_fusion
  373.0 0.6 copy.27
  (9 shorter events, 0.1 us)
Async XLA Ops:
  7.2 58.6 %copy-start.2 = (bf16[1,512]{1,0:T(2,128)(2,1)S(1)}, bf16[1,512]{1,0:T(2,128)(2,1)}, u32[]{:S(2)}) copy-start(bf16[1,512]{1,0:T(2,128)(2,1)} %param.4) | copy-start | bytes 3076
  114.2 4.0 %copy-start = (bf16[1,1024,256]{2,1,0:T(8,128)(2,1)S(1)}, bf16[1,1024,256]{2,1,0:T(8,128)(2,1)}, u32[]{:S(2)}) copy-start(bf16[1,1024,256]{2,1,0:T(8,128)(2,1)} %param.6) | copy-start | bytes 1572868
  114.2 44.8 %all-to-all-start = ((bf16[16,64,1024]{2,1,0:T(8,128)(2,1)}), bf16[16,64,1024]{2,1,0:T(8,128)(2,1)S(1)}, u32[]{:S(2)}, u32[]{:S(2)}) async-start(bf16[16,64,1024]{2,1,0:T(8,128)(2,1)} %bitcast.62), calls=%async_computation | async-start | bytes 4194304 | tf_op jit(solution)/shard_map/all_to_all | solution.py:17
  163.9 16.5 %copy-start.1 = (bf16[1024,256]{1,0:T(8,128)(2,1)S(1)}, bf16[1024,256]{1,0:T(8,128)(2,1)}, u32[]{:S(2)}) copy-start(bf16[1024,256]{1,0:T(8,128)(2,1)} %param.7) | copy-start | bytes 1572868
  169.2 25.5 %all-to-all-start.1 = ((bf16[16,2,8192]{2,1,0:T(2,128)(2,1)}), bf16[16,2,8192]{2,1,0:T(2,128)(2,1)S(1)}, u32[]{:S(2)}, u32[]{:S(2)}) async-start(bf16[16,2,8192]{2,1,0:T(2,128)(2,1)} %reshape.121), calls=%async_computation.1 | async-start | bytes 1048576 | tf_op jit(solution)/shard_map/all_to_all | solution.py:40
  180.4 191.8 %all-reduce.2.cloned.1.call-start = ((), (), s32[]{:S(2)}) async-start(), calls=%async_computation.2 | async-start | bytes 131072 | tf_op jit(solution)/shard_map/psum | solution.py:54
Sparse Core Ops, SparseCore 0:
  286.4 85.7 all-reduce.1
where the time goes:
time: 382 us; the launch traced here: 380 us
  waiting for transfers between devices  140 us (37%)
  matrix products  109 us (29%)
  local copies, waits for them, and re-layouts  74.3 us (19%)
  blocking collectives  23.2 us (6%)
  starting transfers between devices  15.3 us (4%)
  between operations  14.2 us (4%)
  other arithmetic  4.9 us (1%)
    psum x1, waiting for transfers between devices, per_device(): summed = lax.psum(partial_value, 'wide')  85 us
    dot_general x1, matrix products, per_device(): jnp.dot(tile_green, chol_flat.T, preferred_element_type=jnp.float32)  80 us
    unnamed x14, local copies, waits for them, and re-layouts  64.8 us
    all_to_all x1, waiting for transfers between devices, per_device(): lax.all_to_all(generator, 'wide', split_axis=0, concat_axis=1, tiled=True)  40.5 us
    all_gather x1, blocking collectives, per_device(): all_fields = lax.all_gather(fields, 'wide', axis=0, tiled=True)  23.2 us
    dot_general x1, matrix products, per_device(): jnp.dot(all_fields, chol_flat, preferred_element_type=jnp.float32)  22.8 us
    all_to_all x1, waiting for transfers between devices, per_device(): lax.all_to_all(new_orbitals, 'wide', split_axis=1, concat_axis=0, tiled=T...  14.1 us
    all_to_all x1, starting transfers between devices, per_device(): lax.all_to_all(new_orbitals, 'wide', split_axis=1, concat_axis=0, tiled=T...  11.2 us
  transfers between devices with their start and end apart: 3, of which 3 were waited for; matrix products, arithmetic and copies ran while one was open for 0% of the time, Pallas kernels for 0%

commit v1 on v0

v1 whole, which is shorter than its diff:
```python
import functools

import jax
import jax.numpy as jnp
from jax import lax
from jax.experimental import pallas as pl
from jax.experimental.pallas import tpu as pltpu
from jax.sharding import PartitionSpec as P

TAYLOR = 4
RI = 8
BF16 = jnp.bfloat16
F32 = jnp.float32


def expand_kernel(f_ref, o_ref):
    walkers, vectors = f_ref.shape
    lane = lax.broadcasted_iota(jnp.int32, (128, 128 * RI), 1)
    row = lax.broadcasted_iota(jnp.int32, (128, 128 * RI), 0)
    repeat = (lane // RI == row).astype(F32).astype(BF16)
    sub = lax.broadcasted_iota(jnp.int32, (RI, 128 * RI), 0)
    keep = lax.broadcasted_iota(jnp.int32, (RI, 128 * RI), 1) % RI == sub
    for b in range(vectors // 128):
        v = jnp.dot(f_ref[:, b * 128 : (b + 1) * 128], repeat, preferred_element_type=F32)
        e = jnp.where(keep[None], v[:, None, :], 0.0)
        o_ref[:, b * 128 * RI : (b + 1) * 128 * RI] = e.reshape(walkers * RI, 128 * RI).astype(BF16)


def expand(f):
    w, g = f.shape
    return pl.pallas_call(
        expand_kernel,
        out_shape=jax.ShapeDtypeStruct((w * RI, g * RI), BF16),
        cost_estimate=pl.CostEstimate(flops=2 * w * g * 128 * RI, bytes_accessed=w * g * RI * RI * 2, transcendentals=0),
        name="expand",
    )(f)


def gen_kernel(fk_ref, x_ref, o_ref):
    vectors, _, n = x_ref.shape
    x = x_ref[...].reshape(vectors * RI, n)
    part = jnp.dot(fk_ref[...], x, preferred_element_type=F32)
    o_ref[...] = part.reshape(o_ref.shape).astype(BF16)


def gen(fk, chol, first, count):
    vectors, _, n = chol.shape
    w = fk.shape[0] // RI
    wb = min(w, 32)
    return pl.pallas_call(
        gen_kernel,
        grid=(count, w // wb),
        in_specs=[
            pl.BlockSpec((wb * RI, vectors * RI), lambda i, k: (k, 0)),
            pl.BlockSpec((vectors, RI, n), lambda i, k: (0, first + i, 0)),
        ],
        out_specs=pl.BlockSpec((wb, RI, n), lambda i, k: (k, i, 0)),
        out_shape=jax.ShapeDtypeStruct((w, count * RI, n), BF16),
        cost_estimate=pl.CostEstimate(
            flops=2 * w * RI * vectors * count * RI * n, bytes_accessed=vectors * count * RI * n * 2, transcendentals=0
        ),
        name=f"gen_{first}_{count}",
    )(fk, chol)


def half_kernel(t_ref, x_ref, o_ref):
    vectors, _, n = x_ref.shape
    x = x_ref[...].reshape(vectors * RI, n)
    p = jnp.dot(x, t_ref[...], preferred_element_type=F32)
    o_ref[...] = p.reshape(o_ref.shape).astype(BF16)


def half(trial, chol, first, count):
    vectors, _, n = chol.shape
    cols = trial.shape[1]
    return pl.pallas_call(
        half_kernel,
        grid=(count,),
        in_specs=[
            pl.BlockSpec((n, cols), lambda i: (0, 0)),
            pl.BlockSpec((vectors, RI, n), lambda i: (0, first + i, 0)),
        ],
        out_specs=pl.BlockSpec((vectors, RI, cols), lambda i: (0, 0, i)),
        out_shape=jax.ShapeDtypeStruct((vectors, RI, count * cols), BF16),
        cost_estimate=pl.CostEstimate(
            flops=2 * vectors * count * RI * n * cols,
            bytes_accessed=vectors * count * RI * (n + cols) * 2,
            transcendentals=0,
        ),
        name=f"half_{first}_{count}",
    )(trial, chol)


def taylor_kernel(*refs, counts):
    g_refs = refs[: len(counts)]
    q0_ref, new_ref, send_ref, total, even, odd = refs[len(counts) :]
    n, cols = q0_ref.shape
    nocc = cols // 2
    owners = g_refs[0].shape[0]
    rows = n // owners
    total[...] = q0_ref[...].astype(F32).reshape(owners, rows, cols)
    source = q0_ref
    for order in range(1, TAYLOR + 1):
        target = (even, odd)[order % 2]
        q = source[...].reshape(n, cols)
        start = 0
        for g_ref, count in zip(g_refs, counts):
            size = count * RI
            p = jnp.dot(g_ref[...].reshape(owners * size, n), q, preferred_element_type=F32)
            p = p.reshape(owners, size, cols) * (1.0 / order)
            term = jnp.concatenate([-p[:, :, nocc:], p[:, :, :nocc]], axis=2)
            total[:, start : start + size] += term
            if order < TAYLOR:
                target[:, start : start + size] = term.astype(BF16)
            start += size
        source = target
    fresh = total[...].astype(BF16)
    new_ref[...] = fresh.reshape(n, cols)
    for b in range(rows // RI):
        send_ref[:, :, b * cols : (b + 1) * cols] = fresh[:, b * RI : (b + 1) * RI]


def taylor(parts, counts, orbitals):
    n, cols = orbitals.shape
    owners = parts[0].shape[0]
    rows = n // owners
    return pl.pallas_call(
        functools.partial(taylor_kernel, counts=counts),
        out_shape=[
            jax.ShapeDtypeStruct((n, cols), BF16),
            jax.ShapeDtypeStruct((owners, RI, rows // RI * cols), BF16),
        ],
        scratch_shapes=[
            pltpu.VMEM((owners, rows, cols), F32),
            pltpu.VMEM((owners, rows, cols), BF16),
            pltpu.VMEM((owners, rows, cols), BF16),
        ],
        cost_estimate=pl.CostEstimate(flops=2 * TAYLOR * n * n * cols, bytes_accessed=n * (n + 3 * cols) * 2, transcendentals=0),
        name="taylor",
    )(*parts, orbitals)


def bias_kernel(*refs, counts):
    n_ref = refs[0]
    h_refs = refs[1 : 1 + len(counts)]
    o_ref, pair = refs[1 + len(counts) :]
    w, _, depth = n_ref.shape
    cols = depth // sum(counts)
    nocc = cols // 2

    @pl.when(pl.program_id(1) == 0)
    def _():
        v = n_ref[...]
        pair[:, 0] = v
        for b in range(depth // cols):
            s = b * cols
            pair[:, 1, :, s : s + nocc] = v[:, :, s + nocc : s + cols]
            pair[:, 1, :, s + nocc : s + cols] = -v[:, :, s : s + nocc]

    both = pair[...].reshape(w * 2 * RI, depth)
    size = h_refs[0].shape[0]
    out = None
    start = 0
    for h_ref, count in zip(h_refs, counts):
        wide = count * cols
        h = h_ref[...].reshape(size * RI, wide)
        part = lax.dot_general(
            h, both[:, start : start + wide], (((1,), (1,)), ((), ())), preferred_element_type=F32
        )
        out = part if out is None else out + part
        start += wide
    lanes = w * 2 * RI
    sub = lax.broadcasted_iota(jnp.int32, (RI, lanes), 0)
    keep = lax.broadcasted_iota(jnp.int32, (RI, lanes), 1) % RI == sub
    out = jnp.where(keep[None], out.reshape(size, RI, lanes), 0.0).sum(axis=1)
    o_ref[...] = out.T.reshape(w * 2, RI, size).sum(axis=1)


def bias(rows, halves, counts):
    w, _, depth = rows.shape
    vectors = halves[0].shape[0]
    size = min(vectors, 256)
    wb = min(w, 16)
    return pl.pallas_call(
        functools.partial(bias_kernel, counts=counts),
        grid=(w // wb, vectors // size),
        in_specs=[pl.BlockSpec((wb, RI, depth), lambda k, i: (k, 0, 0))]
        + [pl.BlockSpec((size, RI, h.shape[2]), lambda k, i: (i, 0, 0)) for h in halves],
        out_specs=pl.BlockSpec((wb * 2, size), lambda k, i: (k, i)),
        out_shape=jax.ShapeDtypeStruct((w * 2, vectors), F32),
        scratch_shapes=[pltpu.VMEM((wb, 2, RI, depth), BF16)],
        cost_estimate=pl.CostEstimate(
            flops=2 * vectors * RI * depth * w * 2 * RI, bytes_accessed=vectors * RI * depth * 2, transcendentals=0
        ),
        name="bias",
    )(rows, *halves)


def splits(groups):
    first = max(1, groups // 4)
    return (first, groups - first) if groups > first else (groups,)


def exchange(v):
    return lax.all_to_all(v, "wide", split_axis=0, concat_axis=0, tiled=True)


def per_device(fields, chol, orbitals, trial):
    owners = lax.axis_size("wide")
    vectors, rows, n = chol.shape
    counts = splits(rows // RI)
    all_fields = exchange(jnp.broadcast_to(fields, (owners,) + fields.shape[1:]))
    spread = expand(all_fields)
    parts = []
    start = 0
    for count in counts:
        parts.append(exchange(gen(spread, chol, start, count)))
        start += count
    halves = []
    start = 0
    for count in counts:
        halves.append(half(trial, chol, start, count))
        start += count
    fresh, send = taylor(parts, counts, orbitals[0])
    partial = bias(exchange(send), halves, counts)
    mine = exchange(partial.reshape(owners, 2, vectors))
    return fresh[None], mine.sum(axis=0, keepdims=True)


def solution(mesh):
    in_specs = (
        P(("groups", "wide"), None),
        P(None, "wide", None),
        P(("groups", "wide"), None, None),
        P(),
    )
    out_specs = (P(("groups", "wide"), None, None), P(("groups", "wide"), None, None))
    return jax.shard_map(
        per_device, mesh=mesh, in_specs=in_specs, out_specs=out_specs, check_vma=False
    )
```

time: 382 us -> 154 us (0.40)
  waiting for transfers between devices: 140 us -> 22.2 us
  matrix products: 109 us -> 0 us
  Pallas kernels: 0 us -> 79.2 us
  local copies, waits for them, and re-layouts: 74.3 us -> 4 us
  between operations: 14.2 us -> 0.68 us
    dot_general x7 -> x0, matrix products: 109 us -> none  [the longest x1 80 us: per_device(): jnp.dot(tile_green, chol_flat.T, preferred_element_type=jnp.float32)]
    psum x1 -> x0, waiting for transfers between devices: 85 us -> none  [per_device(): summed = lax.psum(partial_value, 'wide')]
    pallas_call x0 -> x7, Pallas kernels: none -> 79.2 us  [the longest x2 34.1 us: half(): pl.pallas_call(half_kernel, grid=(count,), in_specs=[pl.BlockSpec((n, col...]
    unnamed x14 -> x9, local copies, waits for them, and re-layouts: 64.8 us -> 2.59 us
    all_to_all x2 -> x3, waiting for transfers between devices: 54.6 us -> 22.2 us  [exchange(): return lax.all_to_all(v, 'wide', split_axis=0, concat_axis=0, tiled=True)]
    all_to_all x0 -> x2, blocking collectives: none -> 26.4 us  [exchange(): return lax.all_to_all(v, 'wide', split_axis=0, concat_axis=0, tiled=True)]
    all_gather x1 -> x0, blocking collectives: 23.2 us -> none  [per_device(): all_fields = lax.all_gather(fields, 'wide', axis=0, tiled=True)]
    another operation x1 -> x0, local copies, waits for them, and re-layouts: 7.78 us -> none  [per_device(): tile_green.reshape(all_walk, rows, 2, width).transpose(0, 2, 1, 3)]
  transfers between devices with their start and end apart: 3 -> 3, of which waited for: 3 -> 1; matrix products, arithmetic and copies ran while one was open for 0% -> 0% of each run, Pallas kernels for 0% -> 34%
where the time goes in v1:
time: 154 us; the launch traced here: 153 us
  Pallas kernels  79.2 us (51%)
  blocking collectives  26.4 us (17%)
  waiting for transfers between devices  22.2 us (14%)
  starting transfers between devices  18.7 us (12%)
  local copies, waits for them, and re-layouts  4 us (3%)
  other arithmetic  2.06 us (1%)
    pallas_call x2, Pallas kernels, half(): pl.pallas_call(half_kernel, grid=(count,), in_specs=[pl.BlockSpec((n, col...  34.1 us
    pallas_call x2, Pallas kernels, gen(): pl.pallas_call(gen_kernel, grid=(count, w // wb), in_specs=[pl.BlockSpec(...  26.6 us
    all_to_all x2, blocking collectives, exchange(): return lax.all_to_all(v, 'wide', split_axis=0, concat_axis=0, tiled=True)  26.4 us
    all_to_all x3, waiting for transfers between devices, exchange(): return lax.all_to_all(v, 'wide', split_axis=0, concat_axis=0, tiled=True)  22.2 us
    all_to_all x3, starting transfers between devices, exchange(): return lax.all_to_all(v, 'wide', split_axis=0, concat_axis=0, tiled=True)  18.7 us
    pallas_call x1, Pallas kernels, bias(): pl.pallas_call(functools.partial(bias_kernel, counts=counts), grid=(w //...  9.75 us
    pallas_call x1, Pallas kernels, taylor(): pl.pallas_call(functools.partial(taylor_kernel, counts=counts), out_shape...  6.62 us
  transfers between devices with their start and end apart: 3, of which 1 were waited for; matrix products, arithmetic and copies ran while one was open for 0% of the time, Pallas kernels for 34%

profile of v1, /device:TPU:0, one launch (start us, length us, event | category | flops | bytes accessed | tf_op | source)
XLA Modules:
  0.0 153.1 jit_solution(9844232109440456165)
XLA Ops:
  0.6 0.7 reduce
  1.4 0.5 broadcast.5
  1.9 0.7 reduce.1
  2.6 13.7 %all_to_all.28 = bf16[16,2,256]{2,1,0:T(2,128)(2,1)S(1)} all-to-all(bf16[16,2,256]{2,1,0:T(2,128)(2,1)S(1)} %reshape.15), channel_id=1, replica_groups=mesh['groups'=2,'wide'=16] {'wide'}, dimensions={0} | all-to-all | bytes 32768 | tf_op jit(solution)/shard_map/all_to_all | solution.py:205
  16.3 0.6 copy.8
  16.9 2.1 %expand.1.fk_ref = bf16[128,4096]{1,0:T(8,128)(2,1)} custom-call(bf16[16,512]{1,0:T(8,128)(2,1)} %bitcast.6), custom_call_target="tpu_custom_call" | custom-call | flops 16777216 | bytes 1048576 | tf_op jit(solution)/shard_map/expand/pallas_call | solution.py:31
  19.0 8.1 %gen_0_2.1 = bf16[16,16,1024]{2,1,0:T(8,128)(2,1)} custom-call(bf16[128,4096]{1,0:T(8,128)(2,1)} %expand.1.fk_ref, bf16[512,64,1024]{2,1,0:T(8,128)(2,1)} %x_ref.7), custom_call_target="tpu_custom_call" | custom-call | flops 2147483648 | bytes 16777216 | tf_op jit(solution)/shard_map/gen_0_2/pallas_call | solution.py:50
  27.2 3.6 %all-to-all-start.1 = ((bf16[16,16,1024]{2,1,0:T(8,128)(2,1)}), bf16[16,16,1024]{2,1,0:T(8,128)(2,1)S(1)}, u32[]{:S(2)}, u32[]{:S(2)}) async-start(bf16[16,16,1024]{2,1,0:T(8,128)(2,1)} %gen_0_2.1), calls=%async_computation.1 | async-start | bytes 1048576 | tf_op jit(solution)/shard_map/all_to_all | solution.py:205
  30.8 18.4 %gen_2_6.1 = bf16[16,48,1024]{2,1,0:T(8,128)(2,1)} custom-call(bf16[128,4096]{1,0:T(8,128)(2,1)} %expand.1.fk_ref, bf16[512,64,1024]{2,1,0:T(8,128)(2,1)} %x_ref.7), custom_call_target="tpu_custom_call" | custom-call | flops 6442450944 | bytes 50331648 | tf_op jit(solution)/shard_map/gen_2_6/pallas_call | solution.py:50
  49.2 0.0 all-to-all-done.1.refs_0_
  49.2 0.0 copy-start.2
  49.2 6.0 %all-to-all-start.2 = ((bf16[16,48,1024]{2,1,0:T(8,128)(2,1)}), bf16[16,48,1024]{2,1,0:T(8,128)(2,1)S(1)}, u32[]{:S(2)}, u32[]{:S(2)}) async-start(bf16[16,48,1024]{2,1,0:T(8,128)(2,1)} %gen_2_6.1), calls=%async_computation.2 | async-start | bytes 3145728 | tf_op jit(solution)/shard_map/all_to_all | solution.py:205
  55.1 9.7 %half_0_2.1.refs_1_ = bf16[512,8,512]{2,1,0:T(8,128)(2,1)} custom-call(bf16[1024,256]{1,0:T(8,128)(2,1)} %t_ref.3, bf16[512,64,1024]{2,1,0:T(8,128)(2,1)} %x_ref.7), custom_call_target="tpu_custom_call" | custom-call | flops 4294967296 | bytes 20971520 | tf_op jit(solution)/shard_map/half_0_2/pallas_call | solution.py:76
  64.8 0.0 copy-done.2
  64.8 22.2 %all-to-all-done.2.refs_1_ = bf16[16,48,1024]{2,1,0:T(8,128)(2,1)S(1)} async-done(((bf16[16,48,1024]{2,1,0:T(8,128)(2,1)}), bf16[16,48,1024]{2,1,0:T(8,128)(2,1)S(1)}, u32[]{:S(2)}, u32[]{:S(2)}) %all-to-all-start.2) | async-done | bytes 1572896 | tf_op jit(solution)/shard_map/all_to_all | solution.py:205
  87.0 0.0 copy-start.1
  87.0 1.2 copy-done.1
  88.2 6.6 %taylor.1 = (bf16[1024,256]{1,0:T(8,128)(2,1)}, bf16[16,8,2048]{2,1,0:T(8,128)(2,1)}) custom-call(bf16[16,16,1024]{2,1,0:T(8,128)(2,1)} %copy-done.2, bf16[16,48,1024]{2,1,0:T(8,128)(2,1)} %copy-done.1, bf16[1024,256]{1,0:T(8,128)(2,1)} %bitcast.8), custom_call_target="tpu_custom_call" | custom-call | flops 2147483648 | bytes 3670016 | tf_op jit(solution)/shard_map/taylor/pallas_call | solution.py:127
  94.8 9.1 %all-to-all-start.3 = ((bf16[16,8,2048]{2,1,0:T(8,128)(2,1)}), bf16[16,8,2048]{2,1,0:T(8,128)(2,1)S(1)}, u32[]{:S(2)}, u32[]{:S(2)}) async-start(bf16[16,8,2048]{2,1,0:T(8,128)(2,1)} %get-tuple-element.5), calls=%async_computation.3 | async-start | bytes 1048576 | tf_op jit(solution)/shard_map/all_to_all | solution.py:205
  103.9 24.5 %half_2_6.1.refs_2_ = bf16[512,8,1536]{2,1,0:T(8,128)(2,1)} custom-call(bf16[1024,256]{1,0:T(8,128)(2,1)} %t_ref.3, bf16[512,64,1024]{2,1,0:T(8,128)(2,1)} %x_ref.7), custom_call_target="tpu_custom_call" | custom-call | flops 12884901888 | bytes 62914560 | tf_op jit(solution)/shard_map/half_2_6/pallas_call | solution.py:76
  128.4 0.0 all-to-all-done.3.refs_0_
  128.4 0.0 copy-start
  128.4 0.8 copy-done
  129.2 9.8 %bias.1 = f32[32,512]{1,0:T(8,128)} custom-call(bf16[16,8,2048]{2,1,0:T(8,128)(2,1)} %copy-done, bf16[512,8,512]{2,1,0:T(8,128)(2,1)} %half_0_2.1.refs_1_, bf16[512,8,1536]{2,1,0:T(8,128)(2,1)} %half_2_6.1.refs_2_), custom_call_target="tpu_custom_call" | custom-call | flops 4294967296 | bytes 16777216 | tf_op jit(solution)/shard_map/bias/pallas_call | solution.py:184
  138.9 0.9 reshape.13
  139.8 12.7 %all_to_all.29 = f32[16,2,512]{2,1,0:T(2,128)S(1)} all-to-all(f32[16,2,512]{2,1,0:T(2,128)S(1)} %reshape.13), channel_id=1, replica_groups=mesh['groups'=2,'wide'=16] {'wide'}, dimensions={0} | all-to-all | bytes 131072 | tf_op jit(solution)/shard_map/all_to_all | solution.py:205
  152.5 0.6 reduce_sum.9
  (3 shorter events, 0.1 us)
Async XLA Ops:
  27.2 22.0 %all-to-all-start.1 = ((bf16[16,16,1024]{2,1,0:T(8,128)(2,1)}), bf16[16,16,1024]{2,1,0:T(8,128)(2,1)S(1)}, u32[]{:S(2)}, u32[]{:S(2)}) async-start(bf16[16,16,1024]{2,1,0:T(8,128)(2,1)} %gen_0_2.1), calls=%async_computation.1 | async-start | bytes 1048576 | tf_op jit(solution)/shard_map/all_to_all | solution.py:205
  49.2 15.6 %copy-start.2 = (bf16[16,16,1024]{2,1,0:T(8,128)(2,1)}, bf16[16,16,1024]{2,1,0:T(8,128)(2,1)S(1)}, u32[]{:S(2)}) copy-start(bf16[16,16,1024]{2,1,0:T(8,128)(2,1)S(1)} %all-to-all-done.1.refs_0_) | copy-start | bytes 1572868
  49.2 37.8 %all-to-all-start.2 = ((bf16[16,48,1024]{2,1,0:T(8,128)(2,1)}), bf16[16,48,1024]{2,1,0:T(8,128)(2,1)S(1)}, u32[]{:S(2)}, u32[]{:S(2)}) async-start(bf16[16,48,1024]{2,1,0:T(8,128)(2,1)} %gen_2_6.1), calls=%async_computation.2 | async-start | bytes 3145728 | tf_op jit(solution)/shard_map/all_to_all | solution.py:205
  87.0 1.2 copy-start.1
  94.8 33.6 %all-to-all-start.3 = ((bf16[16,8,2048]{2,1,0:T(8,128)(2,1)}), bf16[16,8,2048]{2,1,0:T(8,128)(2,1)S(1)}, u32[]{:S(2)}, u32[]{:S(2)}) async-start(bf16[16,8,2048]{2,1,0:T(8,128)(2,1)} %get-tuple-element.5), calls=%async_computation.3 | async-start | bytes 1048576 | tf_op jit(solution)/shard_map/all_to_all | solution.py:205
  128.4 0.8 copy-start

commit v2 on v1

v2 whole, which is shorter than its diff:
```python
import functools

import jax
import jax.numpy as jnp
from jax import lax
from jax.experimental import pallas as pl
from jax.experimental.pallas import tpu as pltpu
from jax.sharding import PartitionSpec as P

TAYLOR = 4
RI = 8
WB = 16
BF16 = jnp.bfloat16
F32 = jnp.float32
MIB = 1 << 20
VMEM = pl.BlockSpec(memory_space=pltpu.VMEM)
HBM = pl.BlockSpec(memory_space=pltpu.HBM)


def grant(mib):
    return pltpu.CompilerParams(vmem_limit_bytes=mib * MIB)


def copies(fields, owners):
    def kernel(f_ref, o_ref):
        o_ref[...] = jnp.broadcast_to(f_ref[...].astype(F32)[:, None, :], o_ref.shape).astype(BF16)

    return pl.pallas_call(
        kernel,
        in_specs=[VMEM],
        out_specs=VMEM,
        out_shape=jax.ShapeDtypeStruct((owners, RI, fields.shape[1]), BF16),
        compiler_params=grant(4),
        name="copies",
    )(fields)


def expand(f):
    w, _, g = f.shape

    def kernel(f_ref, o_ref):
        fields = f_ref[...].astype(F32)[:, 0, :].astype(BF16)
        lane = lax.broadcasted_iota(jnp.int32, (128, 128 * RI), 1)
        row = lax.broadcasted_iota(jnp.int32, (128, 128 * RI), 0)
        repeat = (lane // RI == row).astype(F32).astype(BF16)
        sub = lax.broadcasted_iota(jnp.int32, (RI, 128 * RI), 0)
        keep = lax.broadcasted_iota(jnp.int32, (RI, 128 * RI), 1) % RI == sub
        for b in range(g // 128):
            v = jnp.dot(fields[:, b * 128 : (b + 1) * 128], repeat, preferred_element_type=F32)
            e = jnp.where(keep[None], v[:, None, :], 0.0)
            o_ref[:, b * 128 * RI : (b + 1) * 128 * RI] = e.reshape(w * RI, 128 * RI).astype(BF16)

    return pl.pallas_call(
        kernel,
        in_specs=[VMEM],
        out_specs=VMEM,
        out_shape=jax.ShapeDtypeStruct((w * RI, g * RI), BF16),
        compiler_params=grant(16),
        cost_estimate=pl.CostEstimate(flops=2 * w * g * 128 * RI, bytes_accessed=w * g * RI * RI * 2, transcendentals=0),
        name="expand",
    )(f)


def gen(fk, chol, first, count):
    vectors, _, n = chol.shape
    w = fk.shape[0] // RI
    wb = min(w, WB)
    pieces, slots = 8, 8
    size = vectors // pieces

    def kernel(fk_ref, c_ref, o_ref, held, done, acc, in_sems, out_sems):
        def fetch(group, piece, slot):
            return pltpu.make_async_copy(
                c_ref.at[pl.ds(piece * size, size), pl.ds(pl.multiple_of((first + group) * RI, RI), RI), :],
                held.at[slot],
                in_sems.at[slot],
            )

        def put(group, slot):
            return pltpu.make_async_copy(
                done.at[slot], o_ref.at[:, pl.ds(pl.multiple_of(group * RI, RI), RI), :], out_sems.at[slot]
            )

        for p in range(slots - 1):
            fetch(0, p, p).start()

        def body(group, _):
            for p in range(pieces):
                fetch(group, p, p).wait()
                ahead = (p + slots - 1) % slots
                if p == 0:
                    fetch(group, ahead, ahead).start()
                else:

                    @pl.when(group + 1 < count)
                    def _():
                        fetch(group + 1, ahead, ahead).start()

                x = held[p].reshape(size * RI, n)
                for k in range(w // wb):
                    r = slice(k * wb * RI, (k + 1) * wb * RI)
                    part = jnp.dot(fk_ref[r, p * size * RI : (p + 1) * size * RI], x, preferred_element_type=F32)
                    if p == 0:
                        acc[r] = part
                    else:
                        acc[r] += part
            slot = lax.rem(group, 2)

            @pl.when(group >= 2)
            def _():
                put(group - 2, slot).wait()

            done[slot] = acc[...].reshape(w, RI, n).astype(BF16)
            put(group, slot).start()
            return 0

        lax.fori_loop(0, count, body, 0)
        for group in range(max(0, count - 2), count):
            put(group, group % 2).wait()

    return pl.pallas_call(
        kernel,
        in_specs=[VMEM, HBM],
        out_specs=HBM,
        out_shape=jax.ShapeDtypeStruct((w, count * RI, n), BF16),
        scratch_shapes=[
            pltpu.VMEM((slots, size, RI, n), BF16),
            pltpu.VMEM((2, w, RI, n), BF16),
            pltpu.VMEM((w * RI, n), F32),
            pltpu.SemaphoreType.DMA((slots,)),
            pltpu.SemaphoreType.DMA((2,)),
        ],
        cost_estimate=pl.CostEstimate(
            flops=2 * w * RI * vectors * count * RI * n, bytes_accessed=vectors * count * RI * n * 2, transcendentals=0
        ),
        compiler_params=grant(16 + w // 4),
    )(fk, chol)


def half(trial, chol, first, count):
    vectors, _, n = chol.shape
    cols = trial.shape[1]

    def kernel(t_ref, x_ref, o_ref):
        x = x_ref[...].reshape(vectors * RI, n)
        p = jnp.dot(x, t_ref[...], preferred_element_type=F32)
        o_ref[...] = p.reshape(o_ref.shape).astype(BF16)

    return pl.pallas_call(
        kernel,
        grid=(count,),
        in_specs=[
            pl.BlockSpec((n, cols), lambda i: (0, 0)),
            pl.BlockSpec((vectors, RI, n), lambda i: (0, first + i, 0)),
        ],
        out_specs=pl.BlockSpec((vectors, RI, cols), lambda i: (0, 0, i)),
        out_shape=jax.ShapeDtypeStruct((vectors, RI, count * cols), BF16),
        cost_estimate=pl.CostEstimate(
            flops=2 * vectors * count * RI * n * cols,
            bytes_accessed=vectors * count * RI * (n + cols) * 2,
            transcendentals=0,
        ),
        compiler_params=grant(56),
    )(trial, chol)


def taylor_kernel(*refs, counts):
    g_refs = refs[: len(counts)]
    q0_ref, new_ref, send_ref, total, even, odd = refs[len(counts) :]
    n, cols = q0_ref.shape
    nocc = cols // 2
    owners = g_refs[0].shape[0]
    rows = n // owners
    total[...] = q0_ref[...].astype(F32).reshape(owners, rows, cols)
    source = q0_ref
    for order in range(1, TAYLOR + 1):
        target = (even, odd)[order % 2]
        q = source[...].reshape(n, cols)
        start = 0
        for g_ref, count in zip(g_refs, counts):
            size = count * RI
            p = jnp.dot(g_ref[...].reshape(owners * size, n), q, preferred_element_type=F32)
            p = p.reshape(owners, size, cols) * (1.0 / order)
            term = jnp.concatenate([-p[:, :, nocc:], p[:, :, :nocc]], axis=2)
            total[:, start : start + size] += term
            if order < TAYLOR:
                target[:, start : start + size] = term.astype(BF16)
            start += size
        source = target
    fresh = total[...].astype(BF16)
    new_ref[...] = fresh.reshape(n, cols)
    for b in range(rows // RI):
        send_ref[:, :, b * cols : (b + 1) * cols] = fresh[:, b * RI : (b + 1) * RI]


def taylor(parts, counts, orbitals):
    n, cols = orbitals.shape
    owners = parts[0].shape[0]
    rows = n // owners
    return pl.pallas_call(
        functools.partial(taylor_kernel, counts=counts),
        in_specs=[VMEM] * (len(parts) + 1),
        out_specs=[VMEM, VMEM],
        out_shape=[
            jax.ShapeDtypeStruct((n, cols), BF16),
            jax.ShapeDtypeStruct((owners, RI, rows // RI * cols), BF16),
        ],
        scratch_shapes=[
            pltpu.VMEM((owners, rows, cols), F32),
            pltpu.VMEM((owners, rows, cols), BF16),
            pltpu.VMEM((owners, rows, cols), BF16),
        ],
        cost_estimate=pl.CostEstimate(flops=2 * TAYLOR * n * n * cols, bytes_accessed=n * (n + 3 * cols) * 2, transcendentals=0),
        compiler_params=grant(12),
        name="taylor",
    )(*parts, orbitals)


def bias_kernel(*refs, counts):
    n_ref = refs[0]
    h_refs = refs[1 : 1 + len(counts)]
    o_ref, pair, sems = refs[1 + len(counts) : 4 + len(counts)]
    held = refs[4 + len(counts) :]
    w, _, depth = n_ref.shape
    wb = min(w, WB)
    cols = depth // sum(counts)
    nocc = cols // 2
    vectors = h_refs[0].shape[0]
    pieces = sems.shape[0]
    size = vectors // pieces
    lanes = wb * 2 * RI
    sub = lax.broadcasted_iota(jnp.int32, (RI, lanes), 0)
    keep = lax.broadcasted_iota(jnp.int32, (RI, lanes), 1) % RI == sub

    def fetch(piece, c):
        at = pl.ds(piece * size, size)
        return pltpu.make_async_copy(h_refs[c].at[at], held[c].at[at], sems.at[piece, c])

    for piece in range(pieces):
        for c in range(len(counts)):
            fetch(piece, c).start()

    def block(k, ready):
        for b in range(depth // cols):
            s = b * cols
            real = n_ref[pl.ds(k * wb, wb), :, s : s + cols].astype(F32)
            imag = jnp.concatenate([real[:, :, nocc:], -real[:, :, :nocc]], axis=2)
            pair[:, s : s + cols] = jnp.stack([real, imag], axis=1).reshape(lanes, cols).astype(BF16)
        sums = []
        for piece in range(pieces):
            out = None
            start = 0
            for c, count in enumerate(counts):
                if ready is None:
                    fetch(piece, c).wait()
                wide = count * cols
                h = held[c][piece * size : (piece + 1) * size].reshape(size * RI, wide)
                part = lax.dot_general(
                    h, pair[:, start : start + wide], (((1,), (1,)), ((), ())), preferred_element_type=F32
                )
                out = part if out is None else out + part
                start += wide
            sums.append(jnp.where(keep[None], out.reshape(size, RI, lanes), 0.0).sum(axis=1))
            if len(sums) * size == 128:
                done = jnp.concatenate(sums, axis=0) if len(sums) > 1 else sums[0]
                v = (piece + 1) * size - 128
                o_ref[pl.ds(k * wb, wb), :, v : v + 128] = (
                    done.T.reshape(wb * 2, RI, 128).sum(axis=1).reshape(wb, 2, 128)
                )
                sums = []

    block(0, None)
    if w > wb:
        pl.loop(1, w // wb)(lambda k: block(k, True))


def bias(rows, halves, counts):
    w, _, depth = rows.shape
    vectors = halves[0].shape[0]
    wb = min(w, WB)
    return pl.pallas_call(
        functools.partial(bias_kernel, counts=counts),
        in_specs=[VMEM] + [HBM] * len(halves),
        out_specs=VMEM,
        out_shape=jax.ShapeDtypeStruct((w, 2, vectors), F32),
        scratch_shapes=[
            pltpu.VMEM((wb * 2 * RI, depth), BF16),
            pltpu.SemaphoreType.DMA((vectors // 64, len(halves))),
        ]
        + [pltpu.VMEM(h.shape, BF16) for h in halves],
        cost_estimate=pl.CostEstimate(
            flops=2 * vectors * RI * depth * w * 2 * RI, bytes_accessed=vectors * RI * depth * 2, transcendentals=0
        ),
        compiler_params=grant(56),
        name="bias",
    )(rows, *halves)


def splits(groups):
    first = max(1, 3 * groups // 8)
    return (first, groups - first) if groups > first else (groups,)


def exchange(v):
    return lax.all_to_all(v, "wide", split_axis=0, concat_axis=0, tiled=True)


def per_device(fields, chol, orbitals, trial):
    owners = lax.axis_size("wide")
    rows = chol.shape[1]
    counts = splits(rows // RI)
    everyone = exchange(copies(fields, owners))
    spread = expand(everyone)
    parts = [exchange(gen(spread, chol, 0, counts[0]))]
    if len(counts) > 1:
        more = gen(spread, chol, counts[0], counts[1])
        parts.append(exchange(more))
    halves = []
    start = 0
    for count in counts:
        halves.append(half(trial, chol, start, count))
        start += count
    fresh, send = taylor(parts, counts, orbitals[0])
    rows_all = exchange(send)
    mine = exchange(bias(rows_all, halves, counts))
    return fresh[None], mine.sum(axis=0, keepdims=True)


def solution(mesh):
    in_specs = (
        P(("groups", "wide"), None),
        P(None, "wide", None),
        P(("groups", "wide"), None, None),
        P(),
    )
    out_specs = (P(("groups", "wide"), None, None), P(("groups", "wide"), None, None))
    return jax.shard_map(
        per_device, mesh=mesh, in_specs=in_specs, out_specs=out_specs, check_vma=False
    )
```

time: 154 us -> 145 us (0.942)
  waiting for transfers between devices: 22.2 us -> 16.5 us
  local copies, waits for them, and re-layouts: 4 us -> 1.48 us
  starting transfers between devices: 18.7 us -> 17 us
  blocking collectives: 26.4 us -> 28 us
    all_to_all x3, waiting for transfers between devices: 22.2 us -> 16.5 us  [exchange(): return lax.all_to_all(v, 'wide', split_axis=0, concat_axis=0, tiled=True)]
    all_to_all x3, starting transfers between devices: 18.7 us -> 17 us  [exchange(): return lax.all_to_all(v, 'wide', split_axis=0, concat_axis=0, tiled=True)]
    all_to_all x2, blocking collectives: 26.4 us -> 28 us  [exchange(): return lax.all_to_all(v, 'wide', split_axis=0, concat_axis=0, tiled=True)]
    pallas_call x7 -> x8, Pallas kernels: 79.2 us -> 80.4 us  [the longest x2 36.4 us: half(): pl.pallas_call(kernel, grid=(count,), in_specs=[pl.BlockSpec((n, cols), l...]
  transfers between devices with their start and end apart: 3 -> 3, of which waited for: 1 -> 2; matrix products, arithmetic and copies ran while one was open for 0% -> 0% of each run, Pallas kernels for 34% -> 35%
where the time goes in v2:
time: 145 us
  Pallas kernels  80.4 us (55%)
  blocking collectives  28 us (19%)
  starting transfers between devices  17 us (12%)
  waiting for transfers between devices  16.5 us (11%)
  local copies, waits for them, and re-layouts  1.48 us (1%)
    pallas_call x2, Pallas kernels, half(): pl.pallas_call(kernel, grid=(count,), in_specs=[pl.BlockSpec((n, cols), l...  36.4 us
    all_to_all x2, blocking collectives, exchange(): return lax.all_to_all(v, 'wide', split_axis=0, concat_axis=0, tiled=True)  28 us
    pallas_call x2, Pallas kernels, gen(): pl.pallas_call(kernel, in_specs=[VMEM, HBM], out_specs=HBM, out_shape=jax...  24.7 us
    all_to_all x3, starting transfers between devices, exchange(): return lax.all_to_all(v, 'wide', split_axis=0, concat_axis=0, tiled=True)  17 us
    all_to_all x3, waiting for transfers between devices, exchange(): return lax.all_to_all(v, 'wide', split_axis=0, concat_axis=0, tiled=True)  16.5 us
    pallas_call x1, Pallas kernels, bias(): pl.pallas_call(functools.partial(bias_kernel, counts=counts), in_specs=[V...  14.2 us
    pallas_call x1, Pallas kernels, taylor(): pl.pallas_call(functools.partial(taylor_kernel, counts=counts), in_specs=...  4.72 us
  transfers between devices with their start and end apart: 3, of which 2 were waited for; matrix products, arithmetic and copies ran while one was open for 0% of the time, Pallas kernels for 35%

profile of v2, /device:TPU:0, one launch (start us, length us, event | category | flops | bytes accessed | tf_op | source)
XLA Modules:
  0.0 144.7 jit_solution(13364117145033561169)
XLA Ops:
  0.6 0.0 copy-start
  0.6 0.7 copy-done
  1.3 15.1 %all_to_all.25.f_ref = bf16[16,8,512]{2,1,0:T(8,128)(2,1)S(1)} all-to-all(bf16[16,8,512]{2,1,0:T(8,128)(2,1)S(1)} %copies.1), channel_id=1, replica_groups=mesh['groups'=2,'wide'=16] {'wide'}, dimensions={0} | all-to-all | bytes 262144 | tf_op jit(solution)/shard_map/all_to_all | solution.py:305
  16.4 0.4 expand.1.fk_ref
  16.8 9.9 %shard_map.59 = bf16[16,24,1024]{2,1,0:T(8,128)(2,1)} custom-call(bf16[128,4096]{1,0:T(8,128)(2,1)S(1)} %expand.1.fk_ref, bf16[512,64,1024]{2,1,0:T(8,128)(2,1)} %x_ref.3), custom_call_target="tpu_custom_call" | custom-call | flops 3221225472 | bytes 25165824 | tf_op jit(solution)/shard_map/pallas_call | solution.py:121
  26.7 3.6 %all-to-all-start.1 = ((bf16[16,24,1024]{2,1,0:T(8,128)(2,1)}), bf16[16,24,1024]{2,1,0:T(8,128)(2,1)S(1)}, u32[]{:S(2)}, u32[]{:S(2)}) async-start(bf16[16,24,1024]{2,1,0:T(8,128)(2,1)} %shard_map.59), calls=%async_computation.1 | async-start | bytes 1572864 | tf_op jit(solution)/shard_map/all_to_all | solution.py:305
  30.3 14.8 %shard_map.60 = bf16[16,40,1024]{2,1,0:T(8,128)(2,1)} custom-call(bf16[128,4096]{1,0:T(8,128)(2,1)S(1)} %expand.1.fk_ref, bf16[512,64,1024]{2,1,0:T(8,128)(2,1)} %x_ref.3), custom_call_target="tpu_custom_call" | custom-call | flops 5368709120 | bytes 41943040 | tf_op jit(solution)/shard_map/pallas_call | solution.py:121
  45.2 3.8 %all-to-all-done.1.refs_0_ = bf16[16,24,1024]{2,1,0:T(8,128)(2,1)S(1)} async-done(((bf16[16,24,1024]{2,1,0:T(8,128)(2,1)}), bf16[16,24,1024]{2,1,0:T(8,128)(2,1)S(1)}, u32[]{:S(2)}, u32[]{:S(2)}) %all-to-all-start.1) | async-done | bytes 786464 | tf_op jit(solution)/shard_map/all_to_all | solution.py:305
  49.0 5.3 %all-to-all-start.2 = ((bf16[16,40,1024]{2,1,0:T(8,128)(2,1)}), bf16[16,40,1024]{2,1,0:T(8,128)(2,1)S(1)}, u32[]{:S(2)}, u32[]{:S(2)}) async-start(bf16[16,40,1024]{2,1,0:T(8,128)(2,1)} %shard_map.60), calls=%async_computation.2 | async-start | bytes 2621440 | tf_op jit(solution)/shard_map/all_to_all | solution.py:305
  54.3 0.0 copy-start.1
  54.3 14.5 %shard_map.61.refs_1_ = bf16[512,8,768]{2,1,0:T(8,128)(2,1)} custom-call(bf16[1024,256]{1,0:T(8,128)(2,1)} %t_ref.3, bf16[512,64,1024]{2,1,0:T(8,128)(2,1)} %x_ref.3), custom_call_target="tpu_custom_call" | custom-call | flops 6442450944 | bytes 31457280 | tf_op jit(solution)/shard_map/pallas_call | solution.py:149
  68.8 12.7 %all-to-all-done.2.refs_1_ = bf16[16,40,1024]{2,1,0:T(8,128)(2,1)S(1)} async-done(((bf16[16,40,1024]{2,1,0:T(8,128)(2,1)}), bf16[16,40,1024]{2,1,0:T(8,128)(2,1)S(1)}, u32[]{:S(2)}, u32[]{:S(2)}) %all-to-all-start.2) | async-done | bytes 1310752 | tf_op jit(solution)/shard_map/all_to_all | solution.py:305
  81.6 0.0 copy-done.1
  81.6 4.7 %taylor.1 = (bf16[1024,256]{1,0:T(8,128)(2,1)}, bf16[16,8,2048]{2,1,0:T(8,128)(2,1)}) custom-call(bf16[16,24,1024]{2,1,0:T(8,128)(2,1)S(1)} %all-to-all-done.1.refs_0_, bf16[16,40,1024]{2,1,0:T(8,128)(2,1)S(1)} %all-to-all-done.2.refs_1_, bf16[1024,256]{1,0:T(8,128)(2,1)S(1)} %bitcast.3), custom_call_target="tpu_custom_call" | custom-call | flops 2147483648 | bytes 3670016 | tf_op jit(solution)/shard_map/taylor/pallas_call | solution.py:200
  86.3 8.0 %all-to-all-start.3 = ((bf16[16,8,2048]{2,1,0:T(8,128)(2,1)}), bf16[16,8,2048]{2,1,0:T(8,128)(2,1)S(1)}, u32[]{:S(2)}, u32[]{:S(2)}) async-start(bf16[16,8,2048]{2,1,0:T(8,128)(2,1)} %get-tuple-element.5), calls=%async_computation.3 | async-start | bytes 1048576 | tf_op jit(solution)/shard_map/all_to_all | solution.py:305
  94.3 21.9 %shard_map.62.refs_2_ = bf16[512,8,1280]{2,1,0:T(8,128)(2,1)} custom-call(bf16[1024,256]{1,0:T(8,128)(2,1)} %t_ref.3, bf16[512,64,1024]{2,1,0:T(8,128)(2,1)} %x_ref.3), custom_call_target="tpu_custom_call" | custom-call | flops 10737418240 | bytes 52428800 | tf_op jit(solution)/shard_map/pallas_call | solution.py:149
  116.2 0.0 all-to-all-done.3.refs_0_
  116.2 0.0 copy-start.2
  116.2 0.8 copy-done.2
  117.0 14.2 %bias.1 = f32[16,2,512]{2,1,0:T(2,128)} custom-call(bf16[16,8,2048]{2,1,0:T(8,128)(2,1)} %copy-done.2, bf16[512,8,768]{2,1,0:T(8,128)(2,1)} %shard_map.61.refs_1_, bf16[512,8,1280]{2,1,0:T(8,128)(2,1)} %shard_map.62.refs_2_), custom_call_target="tpu_custom_call" | custom-call | flops 4294967296 | bytes 16777216 | tf_op jit(solution)/shard_map/bias/pallas_call | solution.py:281
  131.2 12.9 %all_to_all.26 = f32[16,2,512]{2,1,0:T(2,128)S(1)} all-to-all(f32[16,2,512]{2,1,0:T(2,128)} %bias.1), channel_id=1, replica_groups=mesh['groups'=2,'wide'=16] {'wide'}, dimensions={0} | all-to-all | bytes 131072 | tf_op jit(solution)/shard_map/all_to_all | solution.py:305
  144.1 0.6 reduce_sum.9
  (1 shorter events, 0.0 us)
Async XLA Ops:
  0.6 0.7 copy-start
  26.7 22.3 %all-to-all-start.1 = ((bf16[16,24,1024]{2,1,0:T(8,128)(2,1)}), bf16[16,24,1024]{2,1,0:T(8,128)(2,1)S(1)}, u32[]{:S(2)}, u32[]{:S(2)}) async-start(bf16[16,24,1024]{2,1,0:T(8,128)(2,1)} %shard_map.59), calls=%async_computation.1 | async-start | bytes 1572864 | tf_op jit(solution)/shard_map/all_to_all | solution.py:305
  49.0 32.6 %all-to-all-start.2 = ((bf16[16,40,1024]{2,1,0:T(8,128)(2,1)}), bf16[16,40,1024]{2,1,0:T(8,128)(2,1)S(1)}, u32[]{:S(2)}, u32[]{:S(2)}) async-start(bf16[16,40,1024]{2,1,0:T(8,128)(2,1)} %shard_map.60), calls=%async_computation.2 | async-start | bytes 2621440 | tf_op jit(solution)/shard_map/all_to_all | solution.py:305
  54.3 27.3 %copy-start.1 = (bf16[1,1024,256]{2,1,0:T(8,128)(2,1)S(1)}, bf16[1,1024,256]{2,1,0:T(8,128)(2,1)}, u32[]{:S(2)}) copy-start(bf16[1,1024,256]{2,1,0:T(8,128)(2,1)} %param.6) | copy-start | bytes 1572868
  86.3 29.9 %all-to-all-start.3 = ((bf16[16,8,2048]{2,1,0:T(8,128)(2,1)}), bf16[16,8,2048]{2,1,0:T(8,128)(2,1)S(1)}, u32[]{:S(2)}, u32[]{:S(2)}) async-start(bf16[16,8,2048]{2,1,0:T(8,128)(2,1)} %get-tuple-element.5), calls=%async_computation.3 | async-start | bytes 1048576 | tf_op jit(solution)/shard_map/all_to_all | solution.py:305
  116.2 0.8 copy-start.2

commit v3 on v2

v3 whole, which is shorter than its diff:
```python
import functools

import jax
import jax.numpy as jnp
from jax import lax
from jax.experimental import pallas as pl
from jax.experimental.pallas import tpu as pltpu
from jax.sharding import PartitionSpec as P

TAYLOR = 4
RI = 8
WB = 16
BF16 = jnp.bfloat16
F32 = jnp.float32
MIB = 1 << 20
VMEM = pl.BlockSpec(memory_space=pltpu.VMEM)
HBM = pl.BlockSpec(memory_space=pltpu.HBM)


def grant(mib):
    return pltpu.CompilerParams(vmem_limit_bytes=mib * MIB)


def copies(fields, owners):
    def kernel(f_ref, o_ref):
        o_ref[...] = jnp.broadcast_to(f_ref[...].astype(F32)[:, None, :], o_ref.shape).astype(BF16)

    return pl.pallas_call(
        kernel,
        in_specs=[VMEM],
        out_specs=VMEM,
        out_shape=jax.ShapeDtypeStruct((owners, RI, fields.shape[1]), BF16),
        compiler_params=grant(4),
        name="copies",
    )(fields)


def expand(f):
    w, _, g = f.shape

    def kernel(f_ref, o_ref):
        fields = f_ref[...].astype(F32)[:, 0, :].astype(BF16)
        lane = lax.broadcasted_iota(jnp.int32, (128, 128 * RI), 1)
        row = lax.broadcasted_iota(jnp.int32, (128, 128 * RI), 0)
        repeat = (lane // RI == row).astype(F32).astype(BF16)
        sub = lax.broadcasted_iota(jnp.int32, (RI, 128 * RI), 0)
        keep = lax.broadcasted_iota(jnp.int32, (RI, 128 * RI), 1) % RI == sub
        for b in range(g // 128):
            v = jnp.dot(fields[:, b * 128 : (b + 1) * 128], repeat, preferred_element_type=F32)
            e = jnp.where(keep[None], v[:, None, :], 0.0)
            o_ref[:, b * 128 * RI : (b + 1) * 128 * RI] = e.reshape(w * RI, 128 * RI).astype(BF16)

    return pl.pallas_call(
        kernel,
        in_specs=[VMEM],
        out_specs=VMEM,
        out_shape=jax.ShapeDtypeStruct((w * RI, g * RI), BF16),
        compiler_params=grant(16),
        cost_estimate=pl.CostEstimate(flops=2 * w * g * 128 * RI, bytes_accessed=w * g * RI * RI * 2, transcendentals=0),
        name="expand",
    )(f)


def gen(fk, chol, trial, first, count, both):
    vectors, _, n = chol.shape
    cols = trial.shape[1]
    w = fk.shape[0] // RI
    wb = min(w, WB)
    pieces, slots = 8, 8
    size = vectors // pieces

    def kernel(fk_ref, c_ref, *refs):
        if both:
            t_ref, o_ref, h_ref, held, done, acc, in_sems, out_sems, side, side_sems = refs
        else:
            o_ref, held, done, acc, in_sems, out_sems = refs

        def fetch(group, piece, slot):
            return pltpu.make_async_copy(
                c_ref.at[pl.ds(piece * size, size), pl.ds(pl.multiple_of((first + group) * RI, RI), RI), :],
                held.at[slot],
                in_sems.at[slot],
            )

        def put(group, slot):
            return pltpu.make_async_copy(
                done.at[slot], o_ref.at[:, pl.ds(pl.multiple_of(group * RI, RI), RI), :], out_sems.at[slot]
            )

        def put_side(group, slot):
            return pltpu.make_async_copy(
                side.at[slot],
                h_ref.at[:, :, pl.ds(pl.multiple_of((first + group) * cols, cols), cols)],
                side_sems.at[slot],
            )

        for p in range(slots - 1):
            fetch(0, p, p).start()

        def body(group, with_side):
            for p in range(pieces):
                fetch(group, p, p).wait()
                ahead = (p + slots - 1) % slots
                if p == 0:
                    fetch(group, ahead, ahead).start()
                else:

                    @pl.when(group + 1 < count)
                    def _():
                        fetch(group + 1, ahead, ahead).start()

                x = held[p].reshape(size * RI, n)
                for k in range(w // wb):
                    r = slice(k * wb * RI, (k + 1) * wb * RI)
                    part = jnp.dot(fk_ref[r, p * size * RI : (p + 1) * size * RI], x, preferred_element_type=F32)
                    if p == 0:
                        acc[r] = part
                    else:
                        acc[r] += part
                if with_side:
                    product = jnp.dot(x, t_ref[...], preferred_element_type=F32)
                    side[group, p * size : (p + 1) * size] = product.reshape(size, RI, cols).astype(BF16)
            slot = lax.rem(group, 2)

            @pl.when(group >= 2)
            def _():
                put(group - 2, slot).wait()

            done[slot] = acc[...].reshape(w, RI, n).astype(BF16)
            put(group, slot).start()
            if with_side:
                put_side(group, group).start()

        if both:
            pl.loop(0, both)(lambda group: body(group, True))
        if both < count:
            pl.loop(both, count)(lambda group: body(group, False))
        for group in range(max(0, count - 2), count):
            put(group, group % 2).wait()
        for group in range(both):
            put_side(group, group).wait()

    rows_out = jax.ShapeDtypeStruct((w, count * RI, n), BF16)
    half_out = jax.ShapeDtypeStruct((vectors, RI, chol.shape[1] // RI * cols), BF16)
    out = pl.pallas_call(
        kernel,
        in_specs=[VMEM, HBM] + [VMEM] * bool(both),
        out_specs=[HBM, HBM] if both else HBM,
        out_shape=[rows_out, half_out] if both else rows_out,
        scratch_shapes=[
            pltpu.VMEM((slots, size, RI, n), BF16),
            pltpu.VMEM((2, w, RI, n), BF16),
            pltpu.VMEM((w * RI, n), F32),
            pltpu.SemaphoreType.DMA((slots,)),
            pltpu.SemaphoreType.DMA((2,)),
        ]
        + ([pltpu.VMEM((both, vectors, RI, cols), BF16), pltpu.SemaphoreType.DMA((both,))] if both else []),
        cost_estimate=pl.CostEstimate(
            flops=2 * w * RI * vectors * count * RI * n, bytes_accessed=vectors * count * RI * n * 2, transcendentals=0
        ),
        compiler_params=grant(56 if both else 16 + w // 4),
    )(fk, chol, *([trial] if both else []))
    return out if both else (out, None)


def half(trial, chol, some, skip):
    vectors, rows, n = chol.shape
    cols = trial.shape[1]
    groups = rows // RI
    start, stop = skip
    count = groups - (stop - start)

    def kernel(t_ref, x_ref, *refs):
        o_ref = refs[-1]
        x = x_ref[...].reshape(vectors * RI, n)
        p = jnp.dot(x, t_ref[...], preferred_element_type=F32)
        o_ref[...] = p.reshape(o_ref.shape).astype(BF16)

    def group(i):
        return jnp.where(i < start, i, i + (stop - start))

    held = some is not None
    return pl.pallas_call(
        kernel,
        grid=(count,),
        in_specs=[
            pl.BlockSpec((n, cols), lambda i: (0, 0)),
            pl.BlockSpec((vectors, RI, n), lambda i: (0, group(i), 0)),
        ]
        + [HBM] * held,
        out_specs=pl.BlockSpec((vectors, RI, cols), lambda i: (0, 0, group(i))),
        out_shape=jax.ShapeDtypeStruct((vectors, RI, groups * cols), BF16),
        input_output_aliases={2: 0} if held else {},
        cost_estimate=pl.CostEstimate(
            flops=2 * vectors * count * RI * n * cols,
            bytes_accessed=vectors * count * RI * (n + cols) * 2,
            transcendentals=0,
        ),
        compiler_params=grant(56),
        name="half",
    )(trial, chol, *([some] if held else []))


def taylor_kernel(*refs, counts):
    g_refs = refs[: len(counts)]
    q0_ref, half_ref, new_ref, send_ref, kept_ref, total, even, odd, sem = refs[len(counts) :]
    keep = pltpu.make_async_copy(half_ref.at[pl.ds(0, kept_ref.shape[0])], kept_ref, sem)
    keep.start()
    n, cols = q0_ref.shape
    nocc = cols // 2
    owners = g_refs[0].shape[0]
    rows = n // owners
    total[...] = q0_ref[...].astype(F32).reshape(owners, rows, cols)
    source = q0_ref
    for order in range(1, TAYLOR + 1):
        target = (even, odd)[order % 2]
        q = source[...].reshape(n, cols)
        start = 0
        for g_ref, count in zip(g_refs, counts):
            size = count * RI
            p = jnp.dot(g_ref[...].reshape(owners * size, n), q, preferred_element_type=F32)
            p = p.reshape(owners, size, cols) * (1.0 / order)
            term = jnp.concatenate([-p[:, :, nocc:], p[:, :, :nocc]], axis=2)
            total[:, start : start + size] += term
            if order < TAYLOR:
                target[:, start : start + size] = term.astype(BF16)
            start += size
        source = target
    fresh = total[...].astype(BF16)
    new_ref[...] = fresh.reshape(n, cols)
    for b in range(rows // RI):
        send_ref[:, :, b * cols : (b + 1) * cols] = fresh[:, b * RI : (b + 1) * RI]
    keep.wait()


def taylor(parts, counts, orbitals, halves):
    kept = (halves.shape[0] // 2,) + halves.shape[1:]
    n, cols = orbitals.shape
    owners = parts[0].shape[0]
    rows = n // owners
    return pl.pallas_call(
        functools.partial(taylor_kernel, counts=counts),
        in_specs=[VMEM] * (len(parts) + 1) + [HBM],
        out_specs=[VMEM] * 3,
        out_shape=[
            jax.ShapeDtypeStruct((n, cols), BF16),
            jax.ShapeDtypeStruct((owners, RI, rows // RI * cols), BF16),
            jax.ShapeDtypeStruct(kept, BF16),
        ],
        scratch_shapes=[
            pltpu.VMEM((owners, rows, cols), F32),
            pltpu.VMEM((owners, rows, cols), BF16),
            pltpu.VMEM((owners, rows, cols), BF16),
            pltpu.SemaphoreType.DMA,
        ],
        cost_estimate=pl.CostEstimate(flops=2 * TAYLOR * n * n * cols, bytes_accessed=n * (n + 3 * cols) * 2, transcendentals=0),
        compiler_params=grant(44),
        name="taylor",
    )(*parts, orbitals, halves)


def bias_kernel(*refs, cols):
    n_ref, k_ref, h_ref, o_ref, pair, rest, sems = refs
    w, _, depth = n_ref.shape
    vectors = h_ref.shape[0]
    wb = min(w, WB)
    nocc = cols // 2
    size = 128
    lanes = wb * 2 * RI
    sub = lax.broadcasted_iota(jnp.int32, (RI, lanes), 0)
    keep = lax.broadcasted_iota(jnp.int32, (RI, lanes), 1) % RI == sub
    kept = k_ref.shape[0]
    dmas = [
        pltpu.make_async_copy(h_ref.at[pl.ds(kept + v, size)], rest.at[pl.ds(v, size)], sems.at[v // size])
        for v in range(0, vectors - kept, size)
    ]
    for dma in dmas:
        dma.start()

    def block(k, fetched):
        for s in range(0, depth, cols):
            real = n_ref[pl.ds(k * wb, wb), :, s : s + cols].astype(F32)
            imag = jnp.concatenate([real[:, :, nocc:], -real[:, :, :nocc]], axis=2)
            pair[s : s + cols, :] = jnp.stack([real, imag], axis=1).reshape(lanes, cols).T.astype(BF16)
        for v in range(0, vectors, size):
            if v >= kept and not fetched:
                dmas[(v - kept) // size].wait()
            h = (k_ref[v : v + size] if v < kept else rest[v - kept : v - kept + size]).reshape(size * RI, depth)
            out = jnp.dot(h, pair[...], preferred_element_type=F32)
            out = jnp.where(keep[None], out.reshape(size, RI, lanes), 0.0).sum(axis=1)
            o_ref[pl.ds(k * wb, wb), :, v : v + size] = (
                out.T.reshape(wb * 2, RI, size).sum(axis=1).reshape(wb, 2, size)
            )

    block(0, False)
    if w > wb:
        pl.loop(1, w // wb)(lambda k: block(k, True))


def bias(rows, kept, halves, cols):
    w, _, depth = rows.shape
    vectors = halves.shape[0]
    wb = min(w, WB)
    return pl.pallas_call(
        functools.partial(bias_kernel, cols=cols),
        in_specs=[VMEM, VMEM, HBM],
        out_specs=VMEM,
        out_shape=jax.ShapeDtypeStruct((w, 2, vectors), F32),
        scratch_shapes=[
            pltpu.VMEM((depth, wb * 2 * RI), BF16),
            pltpu.VMEM((vectors - kept.shape[0],) + halves.shape[1:], BF16),
            pltpu.SemaphoreType.DMA(((vectors - kept.shape[0]) // 128,)),
        ],
        cost_estimate=pl.CostEstimate(
            flops=2 * vectors * RI * depth * w * 2 * RI, bytes_accessed=vectors * RI * depth * 2, transcendentals=0
        ),
        compiler_params=grant(44),
        name="bias",
    )(rows, kept, halves)


def splits(groups):
    first = max(1, 3 * groups // 8)
    return (first, groups - first) if groups > first else (groups,)


def exchange(v):
    return lax.all_to_all(v, "wide", split_axis=0, concat_axis=0, tiled=True)


def per_device(fields, chol, orbitals, trial):
    owners = lax.axis_size("wide")
    groups = chol.shape[1] // RI
    cols = trial.shape[1]
    counts = splits(groups)
    start = counts[0]
    stop = start + (min(2, counts[1]) if len(counts) > 1 else 0)
    everyone = exchange(copies(fields, owners))
    spread = expand(everyone)
    parts = [exchange(gen(spread, chol, trial, 0, counts[0], 0)[0])]
    some = None
    if len(counts) > 1:
        more, some = gen(spread, chol, trial, start, counts[1], stop - start)
        parts.append(exchange(more))
    halves = half(trial, chol, some, (start, stop))
    fresh, send, kept = taylor(parts, counts, orbitals[0], halves)
    rows_all = exchange(send)
    mine = exchange(bias(rows_all, kept, halves, cols))
    return fresh[None], mine.sum(axis=0, keepdims=True)


def solution(mesh):
    in_specs = (
        P(("groups", "wide"), None),
        P(None, "wide", None),
        P(("groups", "wide"), None, None),
        P(),
    )
    out_specs = (P(("groups", "wide"), None, None), P(("groups", "wide"), None, None))
    return jax.shard_map(
        per_device, mesh=mesh, in_specs=in_specs, out_specs=out_specs, check_vma=False
    )
```

time: 145 us -> 141 us (0.972)
  blocking collectives: 28 us -> 48 us
  waiting for transfers between devices: 16.5 us -> 2.84 us
  starting transfers between devices: 17 us -> 9.61 us
  Pallas kernels: 80.4 us -> 74.4 us
  local copies, waits for them, and re-layouts: 1.48 us -> 4.07 us
    all_to_all x2 -> x3, blocking collectives: 28 us -> 48 us  [exchange(): return lax.all_to_all(v, 'wide', split_axis=0, concat_axis=0, tiled=True)]
    all_to_all x3 -> x2, waiting for transfers between devices: 16.5 us -> 2.84 us  [exchange(): return lax.all_to_all(v, 'wide', split_axis=0, concat_axis=0, tiled=True)]
    pallas_call x2 -> x1, Pallas kernels: 36.4 us -> 24.4 us  [half(): pl.pallas_call(kernel, grid=(count,), in_specs=[pl.BlockSpec((n, cols), l...]
    all_to_all x3 -> x2, starting transfers between devices: 17 us -> 9.61 us  [exchange(): return lax.all_to_all(v, 'wide', split_axis=0, concat_axis=0, tiled=True)]
    pallas_call x3, Pallas kernels: 38.9 us -> 42.4 us  [the longest x2 34.8 us: gen(): pl.pallas_call(kernel, in_specs=[VMEM, HBM] + [VMEM] * bool(both), out_sp...]
    unnamed x6 -> x8, local copies, waits for them, and re-layouts: 1.48 us -> 4.07 us
    pallas_call x1, Pallas kernels: 4.72 us -> 7.17 us  [taylor(): pl.pallas_call(functools.partial(taylor_kernel, counts=counts), in_specs=...]
  transfers between devices with their start and end apart: 3 -> 2, of which waited for: 2 -> 1; matrix products, arithmetic and copies ran while one was open for 0% -> 0% of each run, Pallas kernels for 35% -> 35%
where the time goes in v3:
time: 141 us; the launch traced here: 140 us
  Pallas kernels  74.4 us (53%)
  blocking collectives  48 us (34%)
  starting transfers between devices  9.61 us (7%)
  local copies, waits for them, and re-layouts  4.07 us (3%)
  waiting for transfers between devices  2.84 us (2%)
    all_to_all x3, blocking collectives, exchange(): return lax.all_to_all(v, 'wide', split_axis=0, concat_axis=0, tiled=True)  48 us
    pallas_call x2, Pallas kernels, gen(): pl.pallas_call(kernel, in_specs=[VMEM, HBM] + [VMEM] * bool(both), out_sp...  34.8 us
    pallas_call x1, Pallas kernels, half(): pl.pallas_call(kernel, grid=(count,), in_specs=[pl.BlockSpec((n, cols), l...  24.4 us
    all_to_all x2, starting transfers between devices, exchange(): return lax.all_to_all(v, 'wide', split_axis=0, concat_axis=0, tiled=True)  9.61 us
    pallas_call x1, Pallas kernels, bias(): pl.pallas_call(functools.partial(bias_kernel, cols=cols), in_specs=[VMEM,...  7.6 us
    pallas_call x1, Pallas kernels, taylor(): pl.pallas_call(functools.partial(taylor_kernel, counts=counts), in_specs=...  7.17 us
    unnamed x8, local copies, waits for them, and re-layouts  4.07 us
    all_to_all x2, waiting for transfers between devices, exchange(): return lax.all_to_all(v, 'wide', split_axis=0, concat_axis=0, tiled=True)  2.84 us
  transfers between devices with their start and end apart: 2, of which 1 were waited for; matrix products, arithmetic and copies ran while one was open for 0% of the time, Pallas kernels for 35%

profile of v3, /device:TPU:0, one launch (start us, length us, event | category | flops | bytes accessed | tf_op | source)
XLA Modules:
  0.0 140.3 jit_solution(2655716284541882303)
XLA Ops:
  0.6 0.0 copy-start.3
  0.6 0.7 copy-done.3
  1.3 15.1 %all_to_all.25.f_ref = bf16[16,8,512]{2,1,0:T(8,128)(2,1)S(1)} all-to-all(bf16[16,8,512]{2,1,0:T(8,128)(2,1)S(1)} %copies.1), channel_id=1, replica_groups=mesh['groups'=2,'wide'=16] {'wide'}, dimensions={0} | all-to-all | bytes 262144 | tf_op jit(solution)/shard_map/all_to_all | solution.py:328
  16.4 0.4 expand.1.fk_ref
  16.8 0.0 copy-start
  16.8 10.2 %shard_map.59 = bf16[16,24,1024]{2,1,0:T(8,128)(2,1)} custom-call(bf16[128,4096]{1,0:T(8,128)(2,1)S(1)} %expand.1.fk_ref, bf16[512,64,1024]{2,1,0:T(8,128)(2,1)} %x_ref.1), custom_call_target="tpu_custom_call" | custom-call | flops 3221225472 | bytes 25165824 | tf_op jit(solution)/shard_map/pallas_call | solution.py:145
  27.0 0.0 copy-done
  27.0 3.6 %all-to-all-start.1 = ((bf16[16,24,1024]{2,1,0:T(8,128)(2,1)}), bf16[16,24,1024]{2,1,0:T(8,128)(2,1)S(1)}, u32[]{:S(2)}, u32[]{:S(2)}) async-start(bf16[16,24,1024]{2,1,0:T(8,128)(2,1)} %shard_map.59), calls=%async_computation.1 | async-start | bytes 1572864 | tf_op jit(solution)/shard_map/all_to_all | solution.py:328
  30.7 24.6 %shard_map.60 = (bf16[16,40,1024]{2,1,0:T(8,128)(2,1)}, bf16[512,8,2048]{2,1,0:T(8,128)(2,1)}) custom-call(bf16[128,4096]{1,0:T(8,128)(2,1)} %copy-done, bf16[512,64,1024]{2,1,0:T(8,128)(2,1)} %x_ref.1, bf16[1024,256]{1,0:T(8,128)(2,1)} %t_ref.1), custom_call_target="tpu_custom_call" | custom-call | flops 5368709120 | bytes 41943040 | tf_op jit(solution)/shard_map/pallas_call | solution.py:145
  55.3 0.0 all-to-all-done.1.refs_0_
  55.3 6.0 %all-to-all-start.2 = ((bf16[16,40,1024]{2,1,0:T(8,128)(2,1)}), bf16[16,40,1024]{2,1,0:T(8,128)(2,1)S(1)}, u32[]{:S(2)}, u32[]{:S(2)}) async-start(bf16[16,40,1024]{2,1,0:T(8,128)(2,1)} %get-tuple-element.7), calls=%async_computation.2 | async-start | bytes 2621440 | tf_op jit(solution)/shard_map/all_to_all | solution.py:328
  61.3 0.0 copy-start.2
  61.3 24.4 %half.1.refs_3_.refs_2_ = bf16[512,8,2048]{2,1,0:T(8,128)(2,1)} custom-call(bf16[1024,256]{1,0:T(8,128)(2,1)} %t_ref.1, bf16[512,64,1024]{2,1,0:T(8,128)(2,1)} %x_ref.1, bf16[512,8,2048]{2,1,0:T(8,128)(2,1)} %get-tuple-element.8.refs_0_), custom_call_target="tpu_custom_call", output_to_operand_aliasing={{}: (2, {})} | custom-call | flops 12884901888 | bytes 62914560 | tf_op jit(solution)/shard_map/half/pallas_call | solution.py:183
  85.8 2.8 %all-to-all-done.2.refs_1_ = bf16[16,40,1024]{2,1,0:T(8,128)(2,1)S(1)} async-done(((bf16[16,40,1024]{2,1,0:T(8,128)(2,1)}), bf16[16,40,1024]{2,1,0:T(8,128)(2,1)S(1)}, u32[]{:S(2)}, u32[]{:S(2)}) %all-to-all-start.2) | async-done | bytes 1310752 | tf_op jit(solution)/shard_map/all_to_all | solution.py:328
  88.6 0.0 copy-done.2
  88.6 7.2 %taylor.1 = (bf16[1024,256]{1,0:T(8,128)(2,1)}, bf16[16,8,2048]{2,1,0:T(8,128)(2,1)S(1)}, bf16[256,8,2048]{2,1,0:T(8,128)(2,1)}) custom-call(bf16[16,24,1024]{2,1,0:T(8,128)(2,1)S(1)} %all-to-all-done.1.refs_0_, bf16[16,40,1024]{2,1,0:T(8,128)(2,1)S(1)} %all-to-all-done.2.refs_1_, bf16[1024,256]{1,0:T(8,128)(2,1)S(1)} %bitcast.3, ...), custom_call_target="tpu_custom_call" | custom-call | flops 2147483648 | bytes 3670016 | tf_op jit(solution)/shard_map/taylor/pallas_call | solution.py:241
  95.8 22.1 %all_to_all.26.refs_0_ = bf16[16,8,2048]{2,1,0:T(8,128)(2,1)S(1)} all-to-all(bf16[16,8,2048]{2,1,0:T(8,128)(2,1)S(1)} %get-tuple-element.10), channel_id=1, replica_groups=mesh['groups'=2,'wide'=16] {'wide'}, dimensions={0} | all-to-all | bytes 1048576 | tf_op jit(solution)/shard_map/all_to_all | solution.py:328
  117.9 0.0 copy-start.1
  117.9 3.4 %copy-done.1 = bf16[256,8,2048]{2,1,0:T(8,128)(2,1)S(1)} copy-done((bf16[256,8,2048]{2,1,0:T(8,128)(2,1)S(1)}, bf16[256,8,2048]{2,1,0:T(8,128)(2,1)}, u32[]{:S(2)}) %copy-start.1) | copy-done | bytes 8388632
  121.2 7.6 %bias.1 = f32[16,2,512]{2,1,0:T(2,128)S(1)} custom-call(bf16[16,8,2048]{2,1,0:T(8,128)(2,1)S(1)} %all_to_all.26.refs_0_, bf16[256,8,2048]{2,1,0:T(8,128)(2,1)S(1)} %copy-done.1, bf16[512,8,2048]{2,1,0:T(8,128)(2,1)} %half.1.refs_3_.refs_2_), custom_call_target="tpu_custom_call" | custom-call | flops 4294967296 | bytes 16777216 | tf_op jit(solution)/shard_map/bias/pallas_call | solution.py:304
  128.9 10.9 %all_to_all.27 = f32[16,2,512]{2,1,0:T(2,128)S(1)} all-to-all(f32[16,2,512]{2,1,0:T(2,128)S(1)} %bias.1), channel_id=1, replica_groups=mesh['groups'=2,'wide'=16] {'wide'}, dimensions={0} | all-to-all | bytes 131072 | tf_op jit(solution)/shard_map/all_to_all | solution.py:328
  139.7 0.6 reduce_sum.9
  (1 shorter events, 0.0 us)
Async XLA Ops:
  0.6 0.7 copy-start.3
  16.8 10.2 %copy-start = (bf16[128,4096]{1,0:T(8,128)(2,1)}, bf16[128,4096]{1,0:T(8,128)(2,1)S(1)}, u32[]{:S(2)}) copy-start(bf16[128,4096]{1,0:T(8,128)(2,1)S(1)} %expand.1.fk_ref) | copy-start | bytes 3145732
  27.0 28.3 %all-to-all-start.1 = ((bf16[16,24,1024]{2,1,0:T(8,128)(2,1)}), bf16[16,24,1024]{2,1,0:T(8,128)(2,1)S(1)}, u32[]{:S(2)}, u32[]{:S(2)}) async-start(bf16[16,24,1024]{2,1,0:T(8,128)(2,1)} %shard_map.59), calls=%async_computation.1 | async-start | bytes 1572864 | tf_op jit(solution)/shard_map/all_to_all | solution.py:328
  55.3 33.3 %all-to-all-start.2 = ((bf16[16,40,1024]{2,1,0:T(8,128)(2,1)}), bf16[16,40,1024]{2,1,0:T(8,128)(2,1)S(1)}, u32[]{:S(2)}, u32[]{:S(2)}) async-start(bf16[16,40,1024]{2,1,0:T(8,128)(2,1)} %get-tuple-element.7), calls=%async_computation.2 | async-start | bytes 2621440 | tf_op jit(solution)/shard_map/all_to_all | solution.py:328
  61.3 27.3 %copy-start.2 = (bf16[1,1024,256]{2,1,0:T(8,128)(2,1)S(1)}, bf16[1,1024,256]{2,1,0:T(8,128)(2,1)}, u32[]{:S(2)}) copy-start(bf16[1,1024,256]{2,1,0:T(8,128)(2,1)} %param.6) | copy-start | bytes 1572868
  117.9 3.4 %copy-start.1 = (bf16[256,8,2048]{2,1,0:T(8,128)(2,1)S(1)}, bf16[256,8,2048]{2,1,0:T(8,128)(2,1)}, u32[]{:S(2)}) copy-start(bf16[256,8,2048]{2,1,0:T(8,128)(2,1)} %get-tuple-element.11.refs_1_) | copy-start | bytes 25165828

commit v4 on v3

--- a/solution.py
+++ b/solution.py
@@ -66,8 +66,9 @@
     cols = trial.shape[1]
     w = fk.shape[0] // RI
     wb = min(w, WB)
-    pieces, slots = 8, 8
+    pieces = 8
     size = vectors // pieces
+    slots = 2 * pieces if both else pieces
 
     def kernel(fk_ref, c_ref, *refs):
         if both:
@@ -94,22 +95,25 @@
                 side_sems.at[slot],
             )
 
-        for p in range(slots - 1):
+        def base(group):
+            return lax.rem(group, 2) * pieces if both else 0
+
+        for p in range(pieces - 1):
             fetch(0, p, p).start()
 
         def body(group, with_side):
+            here, there = base(group), base(group + 1)
             for p in range(pieces):
-                fetch(group, p, p).wait()
-                ahead = (p + slots - 1) % slots
+                fetch(group, p, here + p).wait()
                 if p == 0:
-                    fetch(group, ahead, ahead).start()
+                    fetch(group, pieces - 1, here + pieces - 1).start()
                 else:
 
                     @pl.when(group + 1 < count)
                     def _():
-                        fetch(group + 1, ahead, ahead).start()
-
-                x = held[p].reshape(size * RI, n)
+                        fetch(group + 1, p - 1, there + p - 1).start()
+
+                x = held[here + p].reshape(size * RI, n)
                 for k in range(w // wb):
                     r = slice(k * wb * RI, (k + 1) * wb * RI)
                     part = jnp.dot(fk_ref[r, p * size * RI : (p + 1) * size * RI], x, preferred_element_type=F32)
@@ -117,9 +121,10 @@
                         acc[r] = part
                     else:
                         acc[r] += part
-                if with_side:
-                    product = jnp.dot(x, t_ref[...], preferred_element_type=F32)
-                    side[group, p * size : (p + 1) * size] = product.reshape(size, RI, cols).astype(BF16)
+            if with_side:
+                x = held[pl.ds(here, pieces)].reshape(vectors * RI, n)
+                product = jnp.dot(x, t_ref[...], preferred_element_type=F32)
+                side[group] = product.reshape(vectors, RI, cols).astype(BF16)
             slot = lax.rem(group, 2)
 
             @pl.when(group >= 2)
@@ -254,7 +259,7 @@
             pltpu.SemaphoreType.DMA,
         ],
         cost_estimate=pl.CostEstimate(flops=2 * TAYLOR * n * n * cols, bytes_accessed=n * (n + 3 * cols) * 2, transcendentals=0),
-        compiler_params=grant(44),
+        compiler_params=grant(36),
         name="taylor",
     )(*parts, orbitals, halves)
 
@@ -314,7 +319,7 @@
         cost_estimate=pl.CostEstimate(
             flops=2 * vectors * RI * depth * w * 2 * RI, bytes_accessed=vectors * RI * depth * 2, transcendentals=0
         ),
-        compiler_params=grant(44),
+        compiler_params=grant(40),
         name="bias",
     )(rows, kept, halves)
 

time: 141 us -> 134 us (0.950)
  local copies, waits for them, and re-layouts: 4.07 us -> 0.69 us
  Pallas kernels: 74.4 us -> 71.1 us
    pallas_call x2, Pallas kernels: 34.8 us -> 30.9 us  [gen(): pl.pallas_call(kernel, in_specs=[VMEM, HBM] + [VMEM] * bool(both), out_sp...]
    unnamed x8 -> x6, local copies, waits for them, and re-layouts: 4.07 us -> 0.69 us
  transfers between devices with their start and end apart: 2 -> 2, of which waited for: 1 -> 1; matrix products, arithmetic and copies ran while one was open for 0% -> 0% of each run, Pallas kernels for 35% -> 34%
where the time goes in v4:
time: 134 us
  Pallas kernels  71.1 us (53%)
  blocking collectives  48 us (36%)
  starting transfers between devices  9.61 us (7%)
  waiting for transfers between devices  2.87 us (2%)
    all_to_all x3, blocking collectives, exchange(): return lax.all_to_all(v, 'wide', split_axis=0, concat_axis=0, tiled=True)  48 us
    pallas_call x2, Pallas kernels, gen(): pl.pallas_call(kernel, in_specs=[VMEM, HBM] + [VMEM] * bool(both), out_sp...  30.9 us
    pallas_call x1, Pallas kernels, half(): pl.pallas_call(kernel, grid=(count,), in_specs=[pl.BlockSpec((n, cols), l...  24.4 us
    all_to_all x2, starting transfers between devices, exchange(): return lax.all_to_all(v, 'wide', split_axis=0, concat_axis=0, tiled=True)  9.61 us
    pallas_call x1, Pallas kernels, taylor(): pl.pallas_call(functools.partial(taylor_kernel, counts=counts), in_specs=...  7.79 us
    pallas_call x1, Pallas kernels, bias(): pl.pallas_call(functools.partial(bias_kernel, cols=cols), in_specs=[VMEM,...  7.6 us
    all_to_all x2, waiting for transfers between devices, exchange(): return lax.all_to_all(v, 'wide', split_axis=0, concat_axis=0, tiled=True)  2.87 us
  transfers between devices with their start and end apart: 2, of which 1 were waited for; matrix products, arithmetic and copies ran while one was open for 0% of the time, Pallas kernels for 34%

profile of v4, /device:TPU:0, one launch (start us, length us, event | category | flops | bytes accessed | tf_op | source)
XLA Modules:
  0.0 133.7 jit_solution(9708115958461198086)
XLA Ops:
  0.6 0.0 copy-start.2
  0.6 0.7 copy-done.2
  1.3 15.1 %all_to_all.25.f_ref = bf16[16,8,512]{2,1,0:T(8,128)(2,1)S(1)} all-to-all(bf16[16,8,512]{2,1,0:T(8,128)(2,1)S(1)} %copies.1), channel_id=1, replica_groups=mesh['groups'=2,'wide'=16] {'wide'}, dimensions={0} | all-to-all | bytes 262144 | tf_op jit(solution)/shard_map/all_to_all | solution.py:333
  16.4 0.4 expand.1.fk_ref
  16.8 0.0 copy-start
  16.8 10.2 %shard_map.59 = bf16[16,24,1024]{2,1,0:T(8,128)(2,1)} custom-call(bf16[128,4096]{1,0:T(8,128)(2,1)S(1)} %expand.1.fk_ref, bf16[512,64,1024]{2,1,0:T(8,128)(2,1)} %x_ref.1), custom_call_target="tpu_custom_call" | custom-call | flops 3221225472 | bytes 25165824 | tf_op jit(solution)/shard_map/pallas_call | solution.py:150
  27.0 0.0 copy-done
  27.0 3.6 %all-to-all-start.1 = ((bf16[16,24,1024]{2,1,0:T(8,128)(2,1)}), bf16[16,24,1024]{2,1,0:T(8,128)(2,1)S(1)}, u32[]{:S(2)}, u32[]{:S(2)}) async-start(bf16[16,24,1024]{2,1,0:T(8,128)(2,1)} %shard_map.59), calls=%async_computation.1 | async-start | bytes 1572864 | tf_op jit(solution)/shard_map/all_to_all | solution.py:333
  30.7 20.7 %shard_map.60 = (bf16[16,40,1024]{2,1,0:T(8,128)(2,1)}, bf16[512,8,2048]{2,1,0:T(8,128)(2,1)}) custom-call(bf16[128,4096]{1,0:T(8,128)(2,1)} %copy-done, bf16[512,64,1024]{2,1,0:T(8,128)(2,1)} %x_ref.1, bf16[1024,256]{1,0:T(8,128)(2,1)} %t_ref.1), custom_call_target="tpu_custom_call" | custom-call | flops 5368709120 | bytes 41943040 | tf_op jit(solution)/shard_map/pallas_call | solution.py:150
  51.4 0.0 all-to-all-done.1.refs_0_
  51.4 6.0 %all-to-all-start.2 = ((bf16[16,40,1024]{2,1,0:T(8,128)(2,1)}), bf16[16,40,1024]{2,1,0:T(8,128)(2,1)S(1)}, u32[]{:S(2)}, u32[]{:S(2)}) async-start(bf16[16,40,1024]{2,1,0:T(8,128)(2,1)} %get-tuple-element.7), calls=%async_computation.2 | async-start | bytes 2621440 | tf_op jit(solution)/shard_map/all_to_all | solution.py:333
  57.4 0.0 copy-start.1
  57.4 24.4 %half.1.refs_3_.refs_2_ = bf16[512,8,2048]{2,1,0:T(8,128)(2,1)} custom-call(bf16[1024,256]{1,0:T(8,128)(2,1)} %t_ref.1, bf16[512,64,1024]{2,1,0:T(8,128)(2,1)} %x_ref.1, bf16[512,8,2048]{2,1,0:T(8,128)(2,1)} %get-tuple-element.8.refs_0_), custom_call_target="tpu_custom_call", output_to_operand_aliasing={{}: (2, {})} | custom-call | flops 12884901888 | bytes 62914560 | tf_op jit(solution)/shard_map/half/pallas_call | solution.py:188
  81.8 2.9 %all-to-all-done.2.refs_1_ = bf16[16,40,1024]{2,1,0:T(8,128)(2,1)S(1)} async-done(((bf16[16,40,1024]{2,1,0:T(8,128)(2,1)}), bf16[16,40,1024]{2,1,0:T(8,128)(2,1)S(1)}, u32[]{:S(2)}, u32[]{:S(2)}) %all-to-all-start.2) | async-done | bytes 1310752 | tf_op jit(solution)/shard_map/all_to_all | solution.py:333
  84.7 0.0 copy-done.1
  84.7 7.8 %taylor.1 = (bf16[1024,256]{1,0:T(8,128)(2,1)}, bf16[16,8,2048]{2,1,0:T(8,128)(2,1)S(1)}, bf16[256,8,2048]{2,1,0:T(8,128)(2,1)S(1)}) custom-call(bf16[16,24,1024]{2,1,0:T(8,128)(2,1)S(1)} %all-to-all-done.1.refs_0_, bf16[16,40,1024]{2,1,0:T(8,128)(2,1)S(1)} %all-to-all-done.2.refs_1_, bf16[1024,256]{1,0:T(8,128)(2,1)S(1)} %bitcast.3, ...), custom_call_target="tpu_custom_call" | custom-call | flops 2147483648 | bytes 3670016 | tf_op jit(solution)/shard_map/taylor/pallas_call | solution.py:246
  92.5 22.1 %all_to_all.26.refs_0_ = bf16[16,8,2048]{2,1,0:T(8,128)(2,1)S(1)} all-to-all(bf16[16,8,2048]{2,1,0:T(8,128)(2,1)S(1)} %get-tuple-element.10), channel_id=1, replica_groups=mesh['groups'=2,'wide'=16] {'wide'}, dimensions={0} | all-to-all | bytes 1048576 | tf_op jit(solution)/shard_map/all_to_all | solution.py:333
  114.6 7.6 %bias.1 = f32[16,2,512]{2,1,0:T(2,128)S(1)} custom-call(bf16[16,8,2048]{2,1,0:T(8,128)(2,1)S(1)} %all_to_all.26.refs_0_, bf16[256,8,2048]{2,1,0:T(8,128)(2,1)S(1)} %get-tuple-element.11.refs_1_, bf16[512,8,2048]{2,1,0:T(8,128)(2,1)} %half.1.refs_3_.refs_2_), custom_call_target="tpu_custom_call" | custom-call | flops 4294967296 | bytes 16777216 | tf_op jit(solution)/shard_map/bias/pallas_call | solution.py:309
  122.2 10.9 %all_to_all.27 = f32[16,2,512]{2,1,0:T(2,128)S(1)} all-to-all(f32[16,2,512]{2,1,0:T(2,128)S(1)} %bias.1), channel_id=1, replica_groups=mesh['groups'=2,'wide'=16] {'wide'}, dimensions={0} | all-to-all | bytes 131072 | tf_op jit(solution)/shard_map/all_to_all | solution.py:333
  133.1 0.6 reduce_sum.9
  (1 shorter events, 0.0 us)
Async XLA Ops:
  0.6 0.7 copy-start.2
  16.8 10.2 %copy-start = (bf16[128,4096]{1,0:T(8,128)(2,1)}, bf16[128,4096]{1,0:T(8,128)(2,1)S(1)}, u32[]{:S(2)}) copy-start(bf16[128,4096]{1,0:T(8,128)(2,1)S(1)} %expand.1.fk_ref) | copy-start | bytes 3145732
  27.0 24.4 %all-to-all-start.1 = ((bf16[16,24,1024]{2,1,0:T(8,128)(2,1)}), bf16[16,24,1024]{2,1,0:T(8,128)(2,1)S(1)}, u32[]{:S(2)}, u32[]{:S(2)}) async-start(bf16[16,24,1024]{2,1,0:T(8,128)(2,1)} %shard_map.59), calls=%async_computation.1 | async-start | bytes 1572864 | tf_op jit(solution)/shard_map/all_to_all | solution.py:333
  51.4 33.3 %all-to-all-start.2 = ((bf16[16,40,1024]{2,1,0:T(8,128)(2,1)}), bf16[16,40,1024]{2,1,0:T(8,128)(2,1)S(1)}, u32[]{:S(2)}, u32[]{:S(2)}) async-start(bf16[16,40,1024]{2,1,0:T(8,128)(2,1)} %get-tuple-element.7), calls=%async_computation.2 | async-start | bytes 2621440 | tf_op jit(solution)/shard_map/all_to_all | solution.py:333
  57.4 27.3 %copy-start.1 = (bf16[1,1024,256]{2,1,0:T(8,128)(2,1)S(1)}, bf16[1,1024,256]{2,1,0:T(8,128)(2,1)}, u32[]{:S(2)}) copy-start(bf16[1,1024,256]{2,1,0:T(8,128)(2,1)} %param.6) | copy-start | bytes 1572868

commit v5 on v4

--- a/solution.py
+++ b/solution.py
@@ -210,7 +210,11 @@
     g_refs = refs[: len(counts)]
     q0_ref, half_ref, new_ref, send_ref, kept_ref, total, even, odd, sem = refs[len(counts) :]
     keep = pltpu.make_async_copy(half_ref.at[pl.ds(0, kept_ref.shape[0])], kept_ref, sem)
-    keep.start()
+
+    @pl.when(lax.axis_index("wide") >= 0)
+    def _():
+        keep.start()
+
     n, cols = q0_ref.shape
     nocc = cols // 2
     owners = g_refs[0].shape[0]
@@ -275,27 +279,35 @@
     sub = lax.broadcasted_iota(jnp.int32, (RI, lanes), 0)
     keep = lax.broadcasted_iota(jnp.int32, (RI, lanes), 1) % RI == sub
     kept = k_ref.shape[0]
-    dmas = [
-        pltpu.make_async_copy(h_ref.at[pl.ds(kept + v, size)], rest.at[pl.ds(v, size)], sems.at[v // size])
-        for v in range(0, vectors - kept, size)
-    ]
-    for dma in dmas:
-        dma.start()
+
+    def fetch(piece):
+        at = pl.ds(piece * size, size)
+        return pltpu.make_async_copy(h_ref.at[pl.ds(kept + piece * size, size)], rest.at[at], sems.at[piece])
+
+    pl.loop(0, (vectors - kept) // size)(lambda piece: fetch(piece).start())
 
     def block(k, fetched):
         for s in range(0, depth, cols):
             real = n_ref[pl.ds(k * wb, wb), :, s : s + cols].astype(F32)
             imag = jnp.concatenate([real[:, :, nocc:], -real[:, :, :nocc]], axis=2)
             pair[s : s + cols, :] = jnp.stack([real, imag], axis=1).reshape(lanes, cols).T.astype(BF16)
-        for v in range(0, vectors, size):
-            if v >= kept and not fetched:
-                dmas[(v - kept) // size].wait()
-            h = (k_ref[v : v + size] if v < kept else rest[v - kept : v - kept + size]).reshape(size * RI, depth)
-            out = jnp.dot(h, pair[...], preferred_element_type=F32)
+
+        def piece(h, v):
+            out = jnp.dot(h.reshape(size * RI, depth), pair[...], preferred_element_type=F32)
             out = jnp.where(keep[None], out.reshape(size, RI, lanes), 0.0).sum(axis=1)
-            o_ref[pl.ds(k * wb, wb), :, v : v + size] = (
+            o_ref[pl.ds(k * wb, wb), :, pl.ds(pl.multiple_of(v, size), size)] = (
                 out.T.reshape(wb * 2, RI, size).sum(axis=1).reshape(wb, 2, size)
             )
+
+        @pl.loop(0, kept // size)
+        def _(i):
+            piece(k_ref[pl.ds(i * size, size)], i * size)
+
+        @pl.loop(0, (vectors - kept) // size)
+        def _(i):
+            if not fetched:
+                fetch(i).wait()
+            piece(rest[pl.ds(i * size, size)], kept + i * size)
 
     block(0, False)
     if w > wb:
@@ -339,7 +351,7 @@
     cols = trial.shape[1]
     counts = splits(groups)
     start = counts[0]
-    stop = start + (min(2, counts[1]) if len(counts) > 1 else 0)
+    stop = start + (min(1, counts[1]) if len(counts) > 1 else 0)
     everyone = exchange(copies(fields, owners))
     spread = expand(everyone)
     parts = [exchange(gen(spread, chol, trial, 0, counts[0], 0)[0])]

time: 134 us -> 130 us (0.970)
  waiting for transfers between devices: 2.87 us -> 0.07 us
  blocking collectives: 48 us -> 46.2 us
    pallas_call x1, Pallas kernels: 24.4 us -> 29.1 us  [half(): pl.pallas_call(kernel, grid=(count,), in_specs=[pl.BlockSpec((n, cols), l...]
    all_to_all x2, waiting for transfers between devices: 2.87 us -> 0.07 us  [exchange(): return lax.all_to_all(v, 'wide', split_axis=0, concat_axis=0, tiled=True)]
    pallas_call x2, Pallas kernels: 30.9 us -> 28.8 us  [gen(): pl.pallas_call(kernel, in_specs=[VMEM, HBM] + [VMEM] * bool(both), out_sp...]
    all_to_all x3, blocking collectives: 48 us -> 46.2 us  [exchange(): return lax.all_to_all(v, 'wide', split_axis=0, concat_axis=0, tiled=True)]
    pallas_call x1, Pallas kernels: 7.6 us -> 5.87 us  [bias(): pl.pallas_call(functools.partial(bias_kernel, cols=cols), in_specs=[VMEM,...]
  transfers between devices with their start and end apart: 2 -> 2, of which waited for: 1 -> 1; matrix products, arithmetic and copies ran while one was open for 0% -> 0% of each run, Pallas kernels for 34% -> 37%
where the time goes in v5:
time: 130 us
  Pallas kernels  72 us (55%)
  blocking collectives  46.2 us (36%)
  starting transfers between devices  9.55 us (7%)
    all_to_all x3, blocking collectives, exchange(): return lax.all_to_all(v, 'wide', split_axis=0, concat_axis=0, tiled=True)  46.2 us
    pallas_call x1, Pallas kernels, half(): pl.pallas_call(kernel, grid=(count,), in_specs=[pl.BlockSpec((n, cols), l...  29.1 us
    pallas_call x2, Pallas kernels, gen(): pl.pallas_call(kernel, in_specs=[VMEM, HBM] + [VMEM] * bool(both), out_sp...  28.8 us
    all_to_all x2, starting transfers between devices, exchange(): return lax.all_to_all(v, 'wide', split_axis=0, concat_axis=0, tiled=True)  9.55 us
    pallas_call x1, Pallas kernels, taylor(): pl.pallas_call(functools.partial(taylor_kernel, counts=counts), in_specs=...  7.8 us
    pallas_call x1, Pallas kernels, bias(): pl.pallas_call(functools.partial(bias_kernel, cols=cols), in_specs=[VMEM,...  5.87 us
  transfers between devices with their start and end apart: 2, of which 1 were waited for; matrix products, arithmetic and copies ran while one was open for 0% of the time, Pallas kernels for 37%

profile of v5, /device:TPU:0, one launch (start us, length us, event | category | flops | bytes accessed | tf_op | source)
XLA Modules:
  0.0 129.8 jit_solution(11222240426349400899)
XLA Ops:
  0.6 0.0 copy-start.2
  0.6 0.7 copy-done.2
  1.3 15.1 %all_to_all.25.f_ref = bf16[16,8,512]{2,1,0:T(8,128)(2,1)S(1)} all-to-all(bf16[16,8,512]{2,1,0:T(8,128)(2,1)S(1)} %copies.1), channel_id=1, replica_groups=mesh['groups'=2,'wide'=16] {'wide'}, dimensions={0} | all-to-all | bytes 262144 | tf_op jit(solution)/shard_map/all_to_all | solution.py:345
  16.4 0.4 expand.1.fk_ref
  16.8 0.0 copy-start
  16.8 10.2 %shard_map.59 = bf16[16,24,1024]{2,1,0:T(8,128)(2,1)} custom-call(bf16[128,4096]{1,0:T(8,128)(2,1)S(1)} %expand.1.fk_ref, bf16[512,64,1024]{2,1,0:T(8,128)(2,1)} %x_ref.1), custom_call_target="tpu_custom_call" | custom-call | flops 3221225472 | bytes 25165824 | tf_op jit(solution)/shard_map/pallas_call | solution.py:150
  27.0 0.0 copy-done
  27.0 3.6 %all-to-all-start.1 = ((bf16[16,24,1024]{2,1,0:T(8,128)(2,1)}), bf16[16,24,1024]{2,1,0:T(8,128)(2,1)S(1)}, u32[]{:S(2)}, u32[]{:S(2)}) async-start(bf16[16,24,1024]{2,1,0:T(8,128)(2,1)} %shard_map.59), calls=%async_computation.1 | async-start | bytes 1572864 | tf_op jit(solution)/shard_map/all_to_all | solution.py:345
  30.7 18.6 %shard_map.60 = (bf16[16,40,1024]{2,1,0:T(8,128)(2,1)}, bf16[512,8,2048]{2,1,0:T(8,128)(2,1)}) custom-call(bf16[128,4096]{1,0:T(8,128)(2,1)} %copy-done, bf16[512,64,1024]{2,1,0:T(8,128)(2,1)} %x_ref.1, bf16[1024,256]{1,0:T(8,128)(2,1)} %t_ref.1), custom_call_target="tpu_custom_call" | custom-call | flops 5368709120 | bytes 41943040 | tf_op jit(solution)/shard_map/pallas_call | solution.py:150
  49.2 0.1 all-to-all-done.1.refs_0_
  49.3 5.9 %all-to-all-start.2 = ((bf16[16,40,1024]{2,1,0:T(8,128)(2,1)}), bf16[16,40,1024]{2,1,0:T(8,128)(2,1)S(1)}, u32[]{:S(2)}, u32[]{:S(2)}) async-start(bf16[16,40,1024]{2,1,0:T(8,128)(2,1)} %get-tuple-element.7), calls=%async_computation.2 | async-start | bytes 2621440 | tf_op jit(solution)/shard_map/all_to_all | solution.py:345
  55.2 0.0 copy-start.1
  55.3 29.1 %half.1.refs_3_.refs_2_ = bf16[512,8,2048]{2,1,0:T(8,128)(2,1)} custom-call(bf16[1024,256]{1,0:T(8,128)(2,1)} %t_ref.1, bf16[512,64,1024]{2,1,0:T(8,128)(2,1)} %x_ref.1, bf16[512,8,2048]{2,1,0:T(8,128)(2,1)} %get-tuple-element.8.refs_0_), custom_call_target="tpu_custom_call", output_to_operand_aliasing={{}: (2, {})} | custom-call | flops 15032385536 | bytes 73400320 | tf_op jit(solution)/shard_map/half/pallas_call | solution.py:188
  84.4 0.0 all-to-all-done.2.refs_1_
  84.4 0.0 copy-done.1
  84.4 7.8 %taylor.1 = (bf16[1024,256]{1,0:T(8,128)(2,1)}, bf16[16,8,2048]{2,1,0:T(8,128)(2,1)S(1)}, bf16[256,8,2048]{2,1,0:T(8,128)(2,1)S(1)}) custom-call(bf16[16,24,1024]{2,1,0:T(8,128)(2,1)S(1)} %all-to-all-done.1.refs_0_, bf16[16,40,1024]{2,1,0:T(8,128)(2,1)S(1)} %all-to-all-done.2.refs_1_, bf16[1024,256]{1,0:T(8,128)(2,1)S(1)} %bitcast.3, ...), custom_call_target="tpu_custom_call" | custom-call | flops 2147483648 | bytes 3670016 | tf_op jit(solution)/shard_map/taylor/pallas_call | solution.py:250
  92.2 20.2 %all_to_all.26.refs_0_ = bf16[16,8,2048]{2,1,0:T(8,128)(2,1)S(1)} all-to-all(bf16[16,8,2048]{2,1,0:T(8,128)(2,1)S(1)} %get-tuple-element.10), channel_id=1, replica_groups=mesh['groups'=2,'wide'=16] {'wide'}, dimensions={0} | all-to-all | bytes 1048576 | tf_op jit(solution)/shard_map/all_to_all | solution.py:345
  112.4 5.9 %bias.1 = f32[16,2,512]{2,1,0:T(2,128)S(1)} custom-call(bf16[16,8,2048]{2,1,0:T(8,128)(2,1)S(1)} %all_to_all.26.refs_0_, bf16[256,8,2048]{2,1,0:T(8,128)(2,1)S(1)} %get-tuple-element.11.refs_1_, bf16[512,8,2048]{2,1,0:T(8,128)(2,1)} %half.1.refs_3_.refs_2_), custom_call_target="tpu_custom_call" | custom-call | flops 4294967296 | bytes 16777216 | tf_op jit(solution)/shard_map/bias/pallas_call | solution.py:321
  118.3 10.9 %all_to_all.27 = f32[16,2,512]{2,1,0:T(2,128)S(1)} all-to-all(f32[16,2,512]{2,1,0:T(2,128)S(1)} %bias.1), channel_id=1, replica_groups=mesh['groups'=2,'wide'=16] {'wide'}, dimensions={0} | all-to-all | bytes 131072 | tf_op jit(solution)/shard_map/all_to_all | solution.py:345
  129.2 0.6 reduce_sum.9
  (1 shorter events, 0.0 us)
Async XLA Ops:
  0.6 0.7 copy-start.2
  16.8 10.2 %copy-start = (bf16[128,4096]{1,0:T(8,128)(2,1)}, bf16[128,4096]{1,0:T(8,128)(2,1)S(1)}, u32[]{:S(2)}) copy-start(bf16[128,4096]{1,0:T(8,128)(2,1)S(1)} %expand.1.fk_ref) | copy-start | bytes 3145732
  27.0 22.3 %all-to-all-start.1 = ((bf16[16,24,1024]{2,1,0:T(8,128)(2,1)}), bf16[16,24,1024]{2,1,0:T(8,128)(2,1)S(1)}, u32[]{:S(2)}, u32[]{:S(2)}) async-start(bf16[16,24,1024]{2,1,0:T(8,128)(2,1)} %shard_map.59), calls=%async_computation.1 | async-start | bytes 1572864 | tf_op jit(solution)/shard_map/all_to_all | solution.py:345
  49.3 35.1 %all-to-all-start.2 = ((bf16[16,40,1024]{2,1,0:T(8,128)(2,1)}), bf16[16,40,1024]{2,1,0:T(8,128)(2,1)S(1)}, u32[]{:S(2)}, u32[]{:S(2)}) async-start(bf16[16,40,1024]{2,1,0:T(8,128)(2,1)} %get-tuple-element.7), calls=%async_computation.2 | async-start | bytes 2621440 | tf_op jit(solution)/shard_map/all_to_all | solution.py:345
  55.2 29.1 %copy-start.1 = (bf16[1,1024,256]{2,1,0:T(8,128)(2,1)S(1)}, bf16[1,1024,256]{2,1,0:T(8,128)(2,1)}, u32[]{:S(2)}) copy-start(bf16[1,1024,256]{2,1,0:T(8,128)(2,1)} %param.6) | copy-start | bytes 1572868

commit v6 on v5

v6 whole, which is shorter than its diff:
```python
import functools

import jax
import jax.numpy as jnp
from jax import lax
from jax.experimental import pallas as pl
from jax.experimental.pallas import tpu as pltpu
from jax.sharding import PartitionSpec as P

TAYLOR = 4
RI = 8
WB = 32
BF16 = jnp.bfloat16
F32 = jnp.float32
MIB = 1 << 20
VMEM = pl.BlockSpec(memory_space=pltpu.VMEM)
HBM = pl.BlockSpec(memory_space=pltpu.HBM)


def grant(mib):
    return pltpu.CompilerParams(vmem_limit_bytes=mib * MIB)


def copies(fields, owners):
    rows = fields.shape[1] // 128

    def kernel(f_ref, o_ref):
        f = f_ref[...].astype(F32)
        f = jnp.concatenate([f[:, b * 128 : (b + 1) * 128] for b in range(rows)], axis=0)
        o_ref[...] = jnp.broadcast_to(f[None], o_ref.shape).astype(BF16)

    return pl.pallas_call(
        kernel,
        in_specs=[VMEM],
        out_specs=VMEM,
        out_shape=jax.ShapeDtypeStruct((owners, rows, 128), BF16),
        compiler_params=grant(4),
        name="copies",
    )(fields)


def expand(f):
    w, g = f.shape[0], f.shape[1] * f.shape[2]

    def kernel(f_ref, o_ref):
        fields = f_ref[...].astype(F32)
        lane = lax.broadcasted_iota(jnp.int32, (128, 128 * RI), 1)
        row = lax.broadcasted_iota(jnp.int32, (128, 128 * RI), 0)
        repeat = (lane // RI == row).astype(F32).astype(BF16)
        sub = lax.broadcasted_iota(jnp.int32, (RI, 128 * RI), 0)
        keep = lax.broadcasted_iota(jnp.int32, (RI, 128 * RI), 1) % RI == sub
        for b in range(g // 128):
            v = jnp.dot(fields[:, b, :].astype(BF16), repeat, preferred_element_type=F32)
            e = jnp.where(keep[None], v[:, None, :], 0.0)
            o_ref[:, b * 128 * RI : (b + 1) * 128 * RI] = e.reshape(w * RI, 128 * RI).astype(BF16)

    return pl.pallas_call(
        kernel,
        in_specs=[VMEM],
        out_specs=VMEM,
        out_shape=jax.ShapeDtypeStruct((w * RI, g * RI), BF16),
        compiler_params=grant(16),
        cost_estimate=pl.CostEstimate(flops=2 * w * g * 128 * RI, bytes_accessed=w * g * RI * RI * 2, transcendentals=0),
        name="expand",
    )(f)


def gen(fk, chol, share, first, count):
    vectors, rows, n = chol.shape
    w = fk.shape[0] // RI
    wb = min(w, WB)
    pieces = 8
    size = vectors // pieces
    slots = 2 * pieces
    ahead = 4

    def kernel(fk_ref, c_ref, o_ref, held, done, acc, in_sems, out_sems):
        base = first + share.first_group(rows)

        def fetch(group, piece):
            slot = lax.rem(group, 2) * pieces + piece
            return pltpu.make_async_copy(
                c_ref.at[pl.ds(piece * size, size), pl.ds(pl.multiple_of((base + group) * RI, RI), RI), :],
                held.at[slot],
                in_sems.at[slot],
            )

        def put(group, slot):
            return pltpu.make_async_copy(
                done.at[slot], o_ref.at[:, pl.ds(pl.multiple_of(group * RI, RI), RI), :], out_sems.at[slot]
            )

        for p in range(min(ahead, count * pieces)):
            fetch(p // pieces, p % pieces).start()

        @pl.loop(0, count)
        def _(group):
            for p in range(pieces):
                fetch(group, p).wait()
                later, piece = divmod(p + ahead, pieces)

                @pl.when(group + later < count)
                def _():
                    fetch(group + later, piece).start()

                x = held[lax.rem(group, 2) * pieces + p].reshape(size * RI, n)
                for k in range(w // wb):
                    r = slice(k * wb * RI, (k + 1) * wb * RI)
                    part = jnp.dot(fk_ref[r, p * size * RI : (p + 1) * size * RI], x, preferred_element_type=F32)
                    if p == 0:
                        acc[r] = part
                    else:
                        acc[r] += part
            slot = lax.rem(group, 2)

            @pl.when(group >= 2)
            def _():
                put(group - 2, slot).wait()

            done[slot] = acc[...].reshape(w, RI, n).astype(BF16)
            put(group, slot).start()

        for group in range(max(0, count - 2), count):
            put(group, group % 2).wait()

    return pl.pallas_call(
        kernel,
        in_specs=[VMEM, HBM],
        out_specs=HBM,
        out_shape=jax.ShapeDtypeStruct((w, count * RI, n), BF16),
        scratch_shapes=[
            pltpu.VMEM((slots, size, RI, n), BF16),
            pltpu.VMEM((2, w, RI, n), BF16),
            pltpu.VMEM((w * RI, n), F32),
            pltpu.SemaphoreType.DMA((slots,)),
            pltpu.SemaphoreType.DMA((2,)),
        ],
        cost_estimate=pl.CostEstimate(
            flops=2 * w * RI * vectors * count * RI * n, bytes_accessed=vectors * count * RI * n * 2, transcendentals=0
        ),
        compiler_params=grant(56 if first else 24 + w // 8),
    )(fk, chol)


def half(trial, chol):
    vectors, rows, n = chol.shape
    cols = trial.shape[1]
    count = rows // RI

    def kernel(t_ref, x_ref, o_ref):
        x = x_ref[...].reshape(vectors * RI, n)
        p = jnp.dot(x, t_ref[...], preferred_element_type=F32)
        o_ref[...] = p.reshape(o_ref.shape).astype(BF16)

    return pl.pallas_call(
        kernel,
        grid=(count,),
        in_specs=[
            pl.BlockSpec((n, cols), lambda i: (0, 0)),
            pl.BlockSpec((vectors, RI, n), lambda i: (0, i, 0)),
        ],
        out_specs=pl.BlockSpec((vectors, RI, cols), lambda i: (0, 0, i)),
        out_shape=jax.ShapeDtypeStruct((vectors, RI, count * cols), BF16),
        cost_estimate=pl.CostEstimate(
            flops=2 * vectors * count * RI * n * cols,
            bytes_accessed=vectors * count * RI * (n + cols) * 2,
            transcendentals=0,
        ),
        compiler_params=grant(56),
        name="half",
    )(trial, chol)


def taylor_kernel(*refs, counts, parts):
    g_refs = refs[: len(counts)]
    q0_ref, half_ref, new_ref, send_ref, kept_ref, total, even, odd, sems = refs[len(counts) :]
    piece = kept_ref.shape[0] // sems.shape[0]

    def keep(i):
        at = pl.ds(i * piece, piece)
        return pltpu.make_async_copy(half_ref.at[at], kept_ref.at[at], sems.at[i])

    pl.loop(0, sems.shape[0])(lambda i: keep(i).start())
    n, cols = q0_ref.shape
    nocc = cols // 2
    senders = g_refs[0].shape[0]
    owners = senders // parts
    rows = n // owners
    total[...] = q0_ref[...].astype(F32).reshape(owners, rows, cols)
    source = q0_ref
    for order in range(1, TAYLOR + 1):
        target = (even, odd)[order % 2]
        q = source[...].reshape(n, cols)
        start = 0
        for g_ref, count in zip(g_refs, counts):
            size = count * RI
            p = jnp.dot(g_ref[...].reshape(senders * size, n), q, preferred_element_type=F32)
            p = p.reshape(senders, size, cols) * (1.0 / order)
            term = jnp.concatenate([-p[:, :, nocc:], p[:, :, :nocc]], axis=2)
            for part in range(parts):
                mine = term[part * owners : (part + 1) * owners]
                at = part * (rows // parts) + start
                total[:, at : at + size] += mine
                if order < TAYLOR:
                    target[:, at : at + size] = mine.astype(BF16)
            start += size
        source = target
    fresh = total[...].astype(BF16)
    new_ref[...] = fresh.reshape(n, cols)
    for b in range(rows // RI):
        send_ref[:, :, b * cols : (b + 1) * cols] = fresh[:, b * RI : (b + 1) * RI]
    pl.loop(0, sems.shape[0])(lambda i: keep(i).wait())


def taylor(received, counts, parts, orbitals, halves):
    kept = (halves.shape[0] // 2,) + halves.shape[1:]
    n, cols = orbitals.shape
    senders = received[0].shape[0]
    owners = senders // parts
    rows = n // owners
    return pl.pallas_call(
        functools.partial(taylor_kernel, counts=counts, parts=parts),
        in_specs=[VMEM] * (len(received) + 1) + [HBM],
        out_specs=[VMEM] * 3,
        out_shape=[
            jax.ShapeDtypeStruct((n, cols), BF16),
            jax.ShapeDtypeStruct((owners, RI, rows // RI * cols), BF16),
            jax.ShapeDtypeStruct(kept, BF16),
        ],
        scratch_shapes=[
            pltpu.VMEM((owners, rows, cols), F32),
            pltpu.VMEM((owners, rows, cols), BF16),
            pltpu.VMEM((owners, rows, cols), BF16),
            pltpu.SemaphoreType.DMA((8,)),
        ],
        cost_estimate=pl.CostEstimate(flops=2 * TAYLOR * n * n * cols, bytes_accessed=n * (n + 3 * cols) * 2, transcendentals=0),
        compiler_params=grant(36),
        name="taylor",
    )(*received, orbitals, halves)


def bias_kernel(*refs, cols):
    n_ref, k_ref, h_ref, o_ref, pair, rest, sems = refs
    w, _, depth = n_ref.shape
    vectors = h_ref.shape[0]
    wb = min(w, WB)
    nocc = cols // 2
    size = 128
    lanes = wb * 2 * RI
    sub = lax.broadcasted_iota(jnp.int32, (RI, lanes), 0)
    keep = lax.broadcasted_iota(jnp.int32, (RI, lanes), 1) % RI == sub
    kept = k_ref.shape[0]

    def fetch(piece):
        at = pl.ds(piece * size, size)
        return pltpu.make_async_copy(h_ref.at[pl.ds(kept + piece * size, size)], rest.at[at], sems.at[piece])

    pl.loop(0, (vectors - kept) // size)(lambda piece: fetch(piece).start())

    def block(k, fetched):
        for s in range(0, depth, cols):
            real = n_ref[pl.ds(k * wb, wb), :, s : s + cols].astype(F32)
            imag = jnp.concatenate([real[:, :, nocc:], -real[:, :, :nocc]], axis=2)
            pair[s : s + cols, :] = jnp.stack([real, imag], axis=1).reshape(lanes, cols).T.astype(BF16)

        def piece(h, v):
            out = jnp.dot(h.reshape(size * RI, depth), pair[...], preferred_element_type=F32)
            out = jnp.where(keep[None], out.reshape(size, RI, lanes), 0.0).sum(axis=1)
            o_ref[pl.ds(k * wb, wb), :, pl.ds(pl.multiple_of(v, size), size)] = (
                out.T.reshape(wb * 2, RI, size).sum(axis=1).reshape(wb, 2, size)
            )

        @pl.loop(0, kept // size)
        def _(i):
            piece(k_ref[pl.ds(i * size, size)], i * size)

        @pl.loop(0, (vectors - kept) // size)
        def _(i):
            if not fetched:
                fetch(i).wait()
            piece(rest[pl.ds(i * size, size)], kept + i * size)

    block(0, False)
    if w > wb:
        pl.loop(1, w // wb)(lambda k: block(k, True))


def bias(rows, kept, halves, cols):
    w, _, depth = rows.shape
    vectors = halves.shape[0]
    wb = min(w, WB)
    return pl.pallas_call(
        functools.partial(bias_kernel, cols=cols),
        in_specs=[VMEM, VMEM, HBM],
        out_specs=VMEM,
        out_shape=jax.ShapeDtypeStruct((w, 2, vectors), F32),
        scratch_shapes=[
            pltpu.VMEM((depth, wb * 2 * RI), BF16),
            pltpu.VMEM((vectors - kept.shape[0],) + halves.shape[1:], BF16),
            pltpu.SemaphoreType.DMA(((vectors - kept.shape[0]) // 128,)),
        ],
        cost_estimate=pl.CostEstimate(
            flops=2 * vectors * RI * depth * w * 2 * RI, bytes_accessed=vectors * RI * depth * 2, transcendentals=0
        ),
        compiler_params=grant(40),
        name="bias",
    )(rows, kept, halves)


class Share:
    def __init__(self, rows):
        holders = lax.axis_size("groups")
        self.parts = holders if rows // RI % holders == 0 else 1
        self.axes = ("groups", "wide") if self.parts > 1 else "wide"
        self.senders = self.parts * lax.axis_size("wide")

    def first_group(self, rows):
        return lax.axis_index("groups") * (rows // RI // self.parts) if self.parts > 1 else 0


def exchange(v, axes):
    return lax.all_to_all(v, axes, split_axis=0, concat_axis=0, tiled=True)


def splits(groups):
    first = max(1, groups // 4)
    return (first, groups - first) if groups > first else (groups,)


def per_device(fields, chol, orbitals, trial):
    rows = chol.shape[1]
    share = Share(rows)
    counts = splits(rows // RI // share.parts)
    everyone = exchange(copies(fields, share.senders), share.axes)
    spread = expand(everyone)
    received = []
    start = 0
    for count in counts:
        made = gen(spread, chol, share, start, count)
        received.append(exchange(made, share.axes))
        start += count
    halves = half(trial, chol)
    fresh, send, kept = taylor(received, counts, share.parts, orbitals[0], halves)
    rows_all = exchange(send, "wide")
    mine = exchange(bias(rows_all, kept, halves, trial.shape[1]), "wide")
    return fresh[None], mine.sum(axis=0, keepdims=True)


def solution(mesh):
    in_specs = (
        P(("groups", "wide"), None),
        P(None, "wide", None),
        P(("groups", "wide"), None, None),
        P(),
    )
    out_specs = (P(("groups", "wide"), None, None), P(("groups", "wide"), None, None))
    return jax.shard_map(
        per_device, mesh=mesh, in_specs=in_specs, out_specs=out_specs, check_vma=False
    )
```

time: 130 us -> 122 us (0.938)
  Pallas kernels: 72 us -> 62.3 us
  waiting for transfers between devices: 0.07 us -> 9.54 us
  blocking collectives: 46.2 us -> 42.1 us
  starting transfers between devices: 9.55 us -> 5.61 us
    pallas_call x3, Pallas kernels: 36.5 us -> 24 us  [the longest x2 18.9 us: gen(): pl.pallas_call(kernel, in_specs=[VMEM, HBM], out_specs=HBM, out_shape=jax...]
    all_to_all x2, waiting for transfers between devices: 0.07 us -> 9.54 us  [exchange(): return lax.all_to_all(v, axes, split_axis=0, concat_axis=0, tiled=True)]
    all_to_all x3, blocking collectives: 46.2 us -> 42.1 us  [exchange(): return lax.all_to_all(v, axes, split_axis=0, concat_axis=0, tiled=True)]
    all_to_all x2, starting transfers between devices: 9.55 us -> 5.61 us  [exchange(): return lax.all_to_all(v, axes, split_axis=0, concat_axis=0, tiled=True)]
    pallas_call x1, Pallas kernels: 29.1 us -> 31.7 us  [half(): pl.pallas_call(kernel, grid=(count,), in_specs=[pl.BlockSpec((n, cols), l...]
  transfers between devices with their start and end apart: 2 -> 2, of which waited for: 1 -> 2; matrix products, arithmetic and copies ran while one was open for 0% -> 0% of each run, Pallas kernels for 37% -> 37%
where the time goes in v6:
time: 122 us
  Pallas kernels  62.3 us (51%)
  blocking collectives  42.1 us (35%)
  waiting for transfers between devices  9.54 us (8%)
  starting transfers between devices  5.61 us (5%)
    all_to_all x3, blocking collectives, exchange(): return lax.all_to_all(v, axes, split_axis=0, concat_axis=0, tiled=True)  42.1 us
    pallas_call x1, Pallas kernels, half(): pl.pallas_call(kernel, grid=(count,), in_specs=[pl.BlockSpec((n, cols), l...  31.7 us
    pallas_call x2, Pallas kernels, gen(): pl.pallas_call(kernel, in_specs=[VMEM, HBM], out_specs=HBM, out_shape=jax...  18.9 us
    all_to_all x2, waiting for transfers between devices, exchange(): return lax.all_to_all(v, axes, split_axis=0, concat_axis=0, tiled=True)  9.54 us
    pallas_call x1, Pallas kernels, bias(): pl.pallas_call(functools.partial(bias_kernel, cols=cols), in_specs=[VMEM,...  5.88 us
    all_to_all x2, starting transfers between devices, exchange(): return lax.all_to_all(v, axes, split_axis=0, concat_axis=0, tiled=True)  5.61 us
    pallas_call x1, Pallas kernels, taylor(): pl.pallas_call(functools.partial(taylor_kernel, counts=counts, parts=part...  5.17 us
  transfers between devices with their start and end apart: 2, of which 2 were waited for; matrix products, arithmetic and copies ran while one was open for 0% of the time, Pallas kernels for 37%

profile of v6, /device:TPU:0, one launch (start us, length us, event | category | flops | bytes accessed | tf_op | source)
XLA Modules:
  0.0 121.6 jit_solution(16380265345385102914)
XLA Ops:
  0.6 0.0 copy-start.2
  0.6 0.7 copy-done.2
  1.3 14.4 %all_to_all.25.f_ref = bf16[32,4,128]{2,1,0:T(4,128)(2,1)S(1)} all-to-all(bf16[32,4,128]{2,1,0:T(4,128)(2,1)S(1)} %copies.1), channel_id=1, replica_groups=mesh['groups'=2,'wide'=16] {'groups','wide'}, dimensions={0} | all-to-all | bytes 65536 | tf_op jit(solution)/shard_map/all_to_all | solution.py:322
  15.7 0.7 expand.1.fk_ref
  16.4 0.0 copy-start
  16.4 5.9 %shard_map.59 = bf16[32,8,1024]{2,1,0:T(8,128)(2,1)} custom-call(bf16[256,4096]{1,0:T(8,128)(2,1)S(1)} %expand.1.fk_ref, bf16[512,64,1024]{2,1,0:T(8,128)(2,1)} %x_ref.1), custom_call_target="tpu_custom_call" | custom-call | flops 2147483648 | bytes 8388608 | tf_op jit(solution)/shard_map/pallas_call | solution.py:126
  22.3 0.0 copy-done
  22.3 2.6 %all-to-all-start.1 = ((bf16[32,8,1024]{2,1,0:T(8,128)(2,1)}), bf16[32,8,1024]{2,1,0:T(8,128)(2,1)S(1)}, u32[]{:S(2)}, u32[]{:S(2)}) async-start(bf16[32,8,1024]{2,1,0:T(8,128)(2,1)} %shard_map.59), calls=%async_computation.1 | async-start | bytes 1048576 | tf_op jit(solution)/shard_map/all_to_all | solution.py:322
  24.9 13.0 %shard_map.60 = bf16[32,24,1024]{2,1,0:T(8,128)(2,1)} custom-call(bf16[256,4096]{1,0:T(8,128)(2,1)} %copy-done, bf16[512,64,1024]{2,1,0:T(8,128)(2,1)} %x_ref.1), custom_call_target="tpu_custom_call" | custom-call | flops 6442450944 | bytes 25165824 | tf_op jit(solution)/shard_map/pallas_call | solution.py:126
  37.9 2.9 %all-to-all-done.1.refs_0_ = bf16[32,8,1024]{2,1,0:T(8,128)(2,1)S(1)} async-done(((bf16[32,8,1024]{2,1,0:T(8,128)(2,1)}), bf16[32,8,1024]{2,1,0:T(8,128)(2,1)S(1)}, u32[]{:S(2)}, u32[]{:S(2)}) %all-to-all-start.1) | async-done | bytes 524320 | tf_op jit(solution)/shard_map/all_to_all | solution.py:322
  40.8 3.0 %all-to-all-start.2 = ((bf16[32,24,1024]{2,1,0:T(8,128)(2,1)}), bf16[32,24,1024]{2,1,0:T(8,128)(2,1)S(1)}, u32[]{:S(2)}, u32[]{:S(2)}) async-start(bf16[32,24,1024]{2,1,0:T(8,128)(2,1)} %shard_map.60), calls=%async_computation.2 | async-start | bytes 3145728 | tf_op jit(solution)/shard_map/all_to_all | solution.py:322
  43.8 0.0 copy-start.1
  43.8 31.7 %half.1.refs_3_.refs_2_ = bf16[512,8,2048]{2,1,0:T(8,128)(2,1)} custom-call(bf16[1024,256]{1,0:T(8,128)(2,1)} %t_ref.1, bf16[512,64,1024]{2,1,0:T(8,128)(2,1)} %x_ref.1), custom_call_target="tpu_custom_call" | custom-call | flops 17179869184 | bytes 83886080 | tf_op jit(solution)/shard_map/half/pallas_call | solution.py:155
  75.5 6.7 %all-to-all-done.2.refs_1_ = bf16[32,24,1024]{2,1,0:T(8,128)(2,1)S(1)} async-done(((bf16[32,24,1024]{2,1,0:T(8,128)(2,1)}), bf16[32,24,1024]{2,1,0:T(8,128)(2,1)S(1)}, u32[]{:S(2)}, u32[]{:S(2)}) %all-to-all-start.2) | async-done | bytes 1572896 | tf_op jit(solution)/shard_map/all_to_all | solution.py:322
  82.2 0.0 copy-done.1
  82.2 5.2 %taylor.1 = (bf16[1024,256]{1,0:T(8,128)(2,1)}, bf16[16,8,2048]{2,1,0:T(8,128)(2,1)S(1)}, bf16[256,8,2048]{2,1,0:T(8,128)(2,1)S(1)}) custom-call(bf16[32,8,1024]{2,1,0:T(8,128)(2,1)S(1)} %all-to-all-done.1.refs_0_, bf16[32,24,1024]{2,1,0:T(8,128)(2,1)S(1)} %all-to-all-done.2.refs_1_, bf16[1024,256]{1,0:T(8,128)(2,1)S(1)} %bitcast.3, ...), custom_call_target="tpu_custom_call" | custom-call | flops 2147483648 | bytes 3670016 | tf_op jit(solution)/shard_map/taylor/pallas_call | solution.py:221
  87.4 16.9 %all_to_all.26.refs_0_ = bf16[16,8,2048]{2,1,0:T(8,128)(2,1)S(1)} all-to-all(bf16[16,8,2048]{2,1,0:T(8,128)(2,1)S(1)} %get-tuple-element.6), channel_id=1, replica_groups=mesh['groups'=2,'wide'=16] {'wide'}, dimensions={0} | all-to-all | bytes 1048576 | tf_op jit(solution)/shard_map/all_to_all | solution.py:322
  104.3 5.9 %bias.1 = f32[16,2,512]{2,1,0:T(2,128)S(1)} custom-call(bf16[16,8,2048]{2,1,0:T(8,128)(2,1)S(1)} %all_to_all.26.refs_0_, bf16[256,8,2048]{2,1,0:T(8,128)(2,1)S(1)} %get-tuple-element.7.refs_1_, bf16[512,8,2048]{2,1,0:T(8,128)(2,1)} %half.1.refs_3_.refs_2_), custom_call_target="tpu_custom_call" | custom-call | flops 4294967296 | bytes 16777216 | tf_op jit(solution)/shard_map/bias/pallas_call | solution.py:292
  110.2 10.8 %all_to_all.27 = f32[16,2,512]{2,1,0:T(2,128)S(1)} all-to-all(f32[16,2,512]{2,1,0:T(2,128)S(1)} %bias.1), channel_id=1, replica_groups=mesh['groups'=2,'wide'=16] {'wide'}, dimensions={0} | all-to-all | bytes 131072 | tf_op jit(solution)/shard_map/all_to_all | solution.py:322
  121.0 0.6 reduce_sum.9
  (1 shorter events, 0.0 us)
Async XLA Ops:
  0.6 0.7 copy-start.2
  16.4 5.9 %copy-start = (bf16[256,4096]{1,0:T(8,128)(2,1)}, bf16[256,4096]{1,0:T(8,128)(2,1)S(1)}, u32[]{:S(2)}) copy-start(bf16[256,4096]{1,0:T(8,128)(2,1)S(1)} %expand.1.fk_ref) | copy-start | bytes 6291460
  22.3 18.5 %all-to-all-start.1 = ((bf16[32,8,1024]{2,1,0:T(8,128)(2,1)}), bf16[32,8,1024]{2,1,0:T(8,128)(2,1)S(1)}, u32[]{:S(2)}, u32[]{:S(2)}) async-start(bf16[32,8,1024]{2,1,0:T(8,128)(2,1)} %shard_map.59), calls=%async_computation.1 | async-start | bytes 1048576 | tf_op jit(solution)/shard_map/all_to_all | solution.py:322
  40.8 41.4 %all-to-all-start.2 = ((bf16[32,24,1024]{2,1,0:T(8,128)(2,1)}), bf16[32,24,1024]{2,1,0:T(8,128)(2,1)S(1)}, u32[]{:S(2)}, u32[]{:S(2)}) async-start(bf16[32,24,1024]{2,1,0:T(8,128)(2,1)} %shard_map.60), calls=%async_computation.2 | async-start | bytes 3145728 | tf_op jit(solution)/shard_map/all_to_all | solution.py:322
  43.8 38.4 %copy-start.1 = (bf16[1,1024,256]{2,1,0:T(8,128)(2,1)S(1)}, bf16[1,1024,256]{2,1,0:T(8,128)(2,1)}, u32[]{:S(2)}) copy-start(bf16[1,1024,256]{2,1,0:T(8,128)(2,1)} %param.6) | copy-start | bytes 1572868

commit v7 on v6

--- a/solution.py
+++ b/solution.py
@@ -39,42 +39,35 @@
     )(fields)
 
 
-def expand(f):
-    w, g = f.shape[0], f.shape[1] * f.shape[2]
-
-    def kernel(f_ref, o_ref):
-        fields = f_ref[...].astype(F32)
-        lane = lax.broadcasted_iota(jnp.int32, (128, 128 * RI), 1)
-        row = lax.broadcasted_iota(jnp.int32, (128, 128 * RI), 0)
-        repeat = (lane // RI == row).astype(F32).astype(BF16)
-        sub = lax.broadcasted_iota(jnp.int32, (RI, 128 * RI), 0)
-        keep = lax.broadcasted_iota(jnp.int32, (RI, 128 * RI), 1) % RI == sub
-        for b in range(g // 128):
-            v = jnp.dot(fields[:, b, :].astype(BF16), repeat, preferred_element_type=F32)
-            e = jnp.where(keep[None], v[:, None, :], 0.0)
-            o_ref[:, b * 128 * RI : (b + 1) * 128 * RI] = e.reshape(w * RI, 128 * RI).astype(BF16)
-
-    return pl.pallas_call(
-        kernel,
-        in_specs=[VMEM],
-        out_specs=VMEM,
-        out_shape=jax.ShapeDtypeStruct((w * RI, g * RI), BF16),
-        compiler_params=grant(16),
-        cost_estimate=pl.CostEstimate(flops=2 * w * g * 128 * RI, bytes_accessed=w * g * RI * RI * 2, transcendentals=0),
-        name="expand",
-    )(f)
-
-
-def gen(fk, chol, share, first, count):
+def spread_fields(f_ref, o_ref):
+    w, blocks, width = f_ref.shape
+    fields = f_ref[...].astype(F32)
+    lane = lax.broadcasted_iota(jnp.int32, (width, width * RI), 1)
+    row = lax.broadcasted_iota(jnp.int32, (width, width * RI), 0)
+    repeat = (lane // RI == row).astype(F32).astype(BF16)
+    sub = lax.broadcasted_iota(jnp.int32, (RI, width * RI), 0)
+    keep = lax.broadcasted_iota(jnp.int32, (RI, width * RI), 1) % RI == sub
+    for b in range(blocks):
+        v = jnp.dot(fields[:, b, :].astype(BF16), repeat, preferred_element_type=F32)
+        e = jnp.where(keep[None], v[:, None, :], 0.0)
+        o_ref[:, b * width * RI : (b + 1) * width * RI] = e.reshape(w * RI, width * RI).astype(BF16)
+
+
+def gen(source, chol, share, first, count):
     vectors, rows, n = chol.shape
-    w = fk.shape[0] // RI
+    fresh = source.ndim == 3
+    w = source.shape[0] if fresh else source.shape[0] // RI
     wb = min(w, WB)
-    pieces = 8
+    pieces, ahead = 8, 8
     size = vectors // pieces
     slots = 2 * pieces
-    ahead = 4
-
-    def kernel(fk_ref, c_ref, o_ref, held, done, acc, in_sems, out_sems):
+
+    def kernel(s_ref, c_ref, *refs):
+        if fresh:
+            o_ref, spread_ref, *refs = refs
+        else:
+            o_ref, *refs = refs
+        fk_ref, held, done, acc, in_sems, out_sems, spread_sem = refs
         base = first + share.first_group(rows)
 
         def fetch(group, piece):
@@ -90,8 +83,20 @@
                 done.at[slot], o_ref.at[:, pl.ds(pl.multiple_of(group * RI, RI), RI), :], out_sems.at[slot]
             )
 
-        for p in range(min(ahead, count * pieces)):
-            fetch(p // pieces, p % pieces).start()
+        if not fresh:
+            spread = pltpu.make_async_copy(s_ref, fk_ref, spread_sem)
+            spread.start()
+
+        @pl.loop(0, min(ahead, count * pieces))
+        def _(p):
+            fetch(p // pieces, lax.rem(p, pieces)).start()
+
+        if fresh:
+            spread_fields(s_ref, fk_ref)
+            spread = pltpu.make_async_copy(fk_ref, spread_ref, spread_sem)
+            spread.start()
+        else:
+            spread.wait()
 
         @pl.loop(0, count)
         def _(group):
@@ -122,24 +127,31 @@
 
         for group in range(max(0, count - 2), count):
             put(group, group % 2).wait()
-
-    return pl.pallas_call(
+        if fresh:
+            spread.wait()
+
+    rows_out = jax.ShapeDtypeStruct((w, count * RI, n), BF16)
+    spread_out = jax.ShapeDtypeStruct((w * RI, vectors * RI), BF16)
+    out = pl.pallas_call(
         kernel,
-        in_specs=[VMEM, HBM],
-        out_specs=HBM,
-        out_shape=jax.ShapeDtypeStruct((w, count * RI, n), BF16),
+        in_specs=[VMEM if fresh else HBM, HBM],
+        out_specs=[HBM, HBM] if fresh else HBM,
+        out_shape=[rows_out, spread_out] if fresh else rows_out,
         scratch_shapes=[
+            pltpu.VMEM((w * RI, vectors * RI), BF16),
             pltpu.VMEM((slots, size, RI, n), BF16),
             pltpu.VMEM((2, w, RI, n), BF16),
             pltpu.VMEM((w * RI, n), F32),
             pltpu.SemaphoreType.DMA((slots,)),
             pltpu.SemaphoreType.DMA((2,)),
+            pltpu.SemaphoreType.DMA,
         ],
         cost_estimate=pl.CostEstimate(
             flops=2 * w * RI * vectors * count * RI * n, bytes_accessed=vectors * count * RI * n * 2, transcendentals=0
         ),
-        compiler_params=grant(56 if first else 24 + w // 8),
-    )(fk, chol)
+        compiler_params=grant(58),
+    )(source, chol)
+    return out if fresh else (out, source)
 
 
 def half(trial, chol):
@@ -194,15 +206,16 @@
         start = 0
         for g_ref, count in zip(g_refs, counts):
             size = count * RI
-            p = jnp.dot(g_ref[...].reshape(senders * size, n), q, preferred_element_type=F32)
-            p = p.reshape(senders, size, cols) * (1.0 / order)
-            term = jnp.concatenate([-p[:, :, nocc:], p[:, :, :nocc]], axis=2)
             for part in range(parts):
-                mine = term[part * owners : (part + 1) * owners]
+                g = g_ref[part * owners : (part + 1) * owners].reshape(owners * size, n)
+                p = jnp.dot(g, q, preferred_element_type=F32).reshape(owners, size, cols)
+                if order > 1:
+                    p = p * (1.0 / order)
+                term = jnp.concatenate([-p[:, :, nocc:], p[:, :, :nocc]], axis=2)
                 at = part * (rows // parts) + start
-                total[:, at : at + size] += mine
+                total[:, at : at + size] += term
                 if order < TAYLOR:
-                    target[:, at : at + size] = mine.astype(BF16)
+                    target[:, at : at + size] = term.astype(BF16)
             start += size
         source = target
     fresh = total[...].astype(BF16)
@@ -332,11 +345,11 @@
     share = Share(rows)
     counts = splits(rows // RI // share.parts)
     everyone = exchange(copies(fields, share.senders), share.axes)
-    spread = expand(everyone)
+    source = everyone
     received = []
     start = 0
     for count in counts:
-        made = gen(spread, chol, share, start, count)
+        made, source = gen(source, chol, share, start, count)
         received.append(exchange(made, share.axes))
         start += count
     halves = half(trial, chol)

time: 122 us -> 121 us (level)
  Pallas kernels: 62.3 us -> 59.6 us
  waiting for transfers between devices: 9.54 us -> 11.3 us
    pallas_call x3 -> x2, Pallas kernels: 19.5 us -> 17.7 us  [gen(): pl.pallas_call(kernel, in_specs=[VMEM if fresh else HBM, HBM], out_specs=...]
    all_to_all x2, waiting for transfers between devices: 9.54 us -> 11.3 us  [exchange(): return lax.all_to_all(v, axes, split_axis=0, concat_axis=0, tiled=True)]
  transfers between devices with their start and end apart: 2 -> 2, of which waited for: 2 -> 2; matrix products, arithmetic and copies ran while one was open for 0% -> 0% of each run, Pallas kernels for 37% -> 36%
where the time goes in v7:
time: 121 us; the launch traced here: 120 us
  Pallas kernels  59.6 us (49%)
  blocking collectives  42.1 us (35%)
  waiting for transfers between devices  11.3 us (9%)
  starting transfers between devices  5.31 us (4%)
    all_to_all x3, blocking collectives, exchange(): return lax.all_to_all(v, axes, split_axis=0, concat_axis=0, tiled=True)  42.1 us
    pallas_call x1, Pallas kernels, half(): pl.pallas_call(kernel, grid=(count,), in_specs=[pl.BlockSpec((n, cols), l...  31.7 us
    pallas_call x2, Pallas kernels, gen(): pl.pallas_call(kernel, in_specs=[VMEM if fresh else HBM, HBM], out_specs=...  17.7 us
    all_to_all x2, waiting for transfers between devices, exchange(): return lax.all_to_all(v, axes, split_axis=0, concat_axis=0, tiled=True)  11.3 us
    pallas_call x1, Pallas kernels, bias(): pl.pallas_call(functools.partial(bias_kernel, cols=cols), in_specs=[VMEM,...  5.88 us
    all_to_all x2, starting transfers between devices, exchange(): return lax.all_to_all(v, axes, split_axis=0, concat_axis=0, tiled=True)  5.31 us
    pallas_call x1, Pallas kernels, taylor(): pl.pallas_call(functools.partial(taylor_kernel, counts=counts, parts=part...  4.26 us
  transfers between devices with their start and end apart: 2, of which 2 were waited for; matrix products, arithmetic and copies ran while one was open for 0% of the time, Pallas kernels for 36%

profile of v7, /device:TPU:0, one launch (start us, length us, event | category | flops | bytes accessed | tf_op | source)
XLA Modules:
  0.0 120.4 jit_solution(18168233646236033753)
XLA Ops:
  0.6 0.0 copy-start.1
  0.6 0.7 copy-done.1
  1.3 14.3 %all_to_all.25.s_ref = bf16[32,4,128]{2,1,0:T(4,128)(2,1)} all-to-all(bf16[32,4,128]{2,1,0:T(4,128)(2,1)S(1)} %copies.1), channel_id=1, replica_groups=mesh['groups'=2,'wide'=16] {'groups','wide'}, dimensions={0} | all-to-all | bytes 65536 | tf_op jit(solution)/shard_map/all_to_all | solution.py:335
  15.7 6.5 %shard_map.59 = (bf16[32,8,1024]{2,1,0:T(8,128)(2,1)}, bf16[256,4096]{1,0:T(8,128)(2,1)}) custom-call(bf16[32,4,128]{2,1,0:T(4,128)(2,1)} %all_to_all.25.s_ref, bf16[512,64,1024]{2,1,0:T(8,128)(2,1)} %x_ref.1), custom_call_target="tpu_custom_call" | custom-call | flops 2147483648 | bytes 8388608 | tf_op jit(solution)/shard_map/pallas_call | solution.py:135
  22.2 2.6 %all-to-all-start.1 = ((bf16[32,8,1024]{2,1,0:T(8,128)(2,1)}), bf16[32,8,1024]{2,1,0:T(8,128)(2,1)S(1)}, u32[]{:S(2)}, u32[]{:S(2)}) async-start(bf16[32,8,1024]{2,1,0:T(8,128)(2,1)} %get-tuple-element.7), calls=%async_computation.1 | async-start | bytes 1048576 | tf_op jit(solution)/shard_map/all_to_all | solution.py:335
  24.8 11.2 %shard_map.60 = bf16[32,24,1024]{2,1,0:T(8,128)(2,1)} custom-call(bf16[256,4096]{1,0:T(8,128)(2,1)} %get-tuple-element.8.s_ref, bf16[512,64,1024]{2,1,0:T(8,128)(2,1)} %x_ref.1), custom_call_target="tpu_custom_call" | custom-call | flops 6442450944 | bytes 25165824 | tf_op jit(solution)/shard_map/pallas_call | solution.py:135
  36.1 4.7 %all-to-all-done.1.refs_0_ = bf16[32,8,1024]{2,1,0:T(8,128)(2,1)S(1)} async-done(((bf16[32,8,1024]{2,1,0:T(8,128)(2,1)}), bf16[32,8,1024]{2,1,0:T(8,128)(2,1)S(1)}, u32[]{:S(2)}, u32[]{:S(2)}) %all-to-all-start.1) | async-done | bytes 524320 | tf_op jit(solution)/shard_map/all_to_all | solution.py:335
  40.7 2.7 %all-to-all-start.2 = ((bf16[32,24,1024]{2,1,0:T(8,128)(2,1)}), bf16[32,24,1024]{2,1,0:T(8,128)(2,1)S(1)}, u32[]{:S(2)}, u32[]{:S(2)}) async-start(bf16[32,24,1024]{2,1,0:T(8,128)(2,1)} %shard_map.60), calls=%async_computation.2 | async-start | bytes 3145728 | tf_op jit(solution)/shard_map/all_to_all | solution.py:335
  43.4 0.0 copy-start
  43.4 31.7 %half.1.refs_3_.refs_2_ = bf16[512,8,2048]{2,1,0:T(8,128)(2,1)} custom-call(bf16[1024,256]{1,0:T(8,128)(2,1)} %t_ref.1, bf16[512,64,1024]{2,1,0:T(8,128)(2,1)} %x_ref.1), custom_call_target="tpu_custom_call" | custom-call | flops 17179869184 | bytes 83886080 | tf_op jit(solution)/shard_map/half/pallas_call | solution.py:167
  75.1 6.7 %all-to-all-done.2.refs_1_ = bf16[32,24,1024]{2,1,0:T(8,128)(2,1)S(1)} async-done(((bf16[32,24,1024]{2,1,0:T(8,128)(2,1)}), bf16[32,24,1024]{2,1,0:T(8,128)(2,1)S(1)}, u32[]{:S(2)}, u32[]{:S(2)}) %all-to-all-start.2) | async-done | bytes 1572896 | tf_op jit(solution)/shard_map/all_to_all | solution.py:335
  81.8 0.0 copy-done
  81.8 4.3 %taylor.1 = (bf16[1024,256]{1,0:T(8,128)(2,1)}, bf16[16,8,2048]{2,1,0:T(8,128)(2,1)S(1)}, bf16[256,8,2048]{2,1,0:T(8,128)(2,1)S(1)}) custom-call(bf16[32,8,1024]{2,1,0:T(8,128)(2,1)S(1)} %all-to-all-done.1.refs_0_, bf16[32,24,1024]{2,1,0:T(8,128)(2,1)S(1)} %all-to-all-done.2.refs_1_, bf16[1024,256]{1,0:T(8,128)(2,1)S(1)} %bitcast.3, ...), custom_call_target="tpu_custom_call" | custom-call | flops 2147483648 | bytes 3670016 | tf_op jit(solution)/shard_map/taylor/pallas_call | solution.py:234
  86.1 16.9 %all_to_all.26.refs_0_ = bf16[16,8,2048]{2,1,0:T(8,128)(2,1)S(1)} all-to-all(bf16[16,8,2048]{2,1,0:T(8,128)(2,1)S(1)} %get-tuple-element.10), channel_id=1, replica_groups=mesh['groups'=2,'wide'=16] {'wide'}, dimensions={0} | all-to-all | bytes 1048576 | tf_op jit(solution)/shard_map/all_to_all | solution.py:335
  103.0 5.9 %bias.1 = f32[16,2,512]{2,1,0:T(2,128)S(1)} custom-call(bf16[16,8,2048]{2,1,0:T(8,128)(2,1)S(1)} %all_to_all.26.refs_0_, bf16[256,8,2048]{2,1,0:T(8,128)(2,1)S(1)} %get-tuple-element.11.refs_1_, bf16[512,8,2048]{2,1,0:T(8,128)(2,1)} %half.1.refs_3_.refs_2_), custom_call_target="tpu_custom_call" | custom-call | flops 4294967296 | bytes 16777216 | tf_op jit(solution)/shard_map/bias/pallas_call | solution.py:305
  108.9 10.9 %all_to_all.27 = f32[16,2,512]{2,1,0:T(2,128)S(1)} all-to-all(f32[16,2,512]{2,1,0:T(2,128)S(1)} %bias.1), channel_id=1, replica_groups=mesh['groups'=2,'wide'=16] {'wide'}, dimensions={0} | all-to-all | bytes 131072 | tf_op jit(solution)/shard_map/all_to_all | solution.py:335
  119.8 0.6 reduce_sum.9
  (1 shorter events, 0.0 us)
Async XLA Ops:
  0.6 0.7 copy-start.1
  22.2 18.5 %all-to-all-start.1 = ((bf16[32,8,1024]{2,1,0:T(8,128)(2,1)}), bf16[32,8,1024]{2,1,0:T(8,128)(2,1)S(1)}, u32[]{:S(2)}, u32[]{:S(2)}) async-start(bf16[32,8,1024]{2,1,0:T(8,128)(2,1)} %get-tuple-element.7), calls=%async_computation.1 | async-start | bytes 1048576 | tf_op jit(solution)/shard_map/all_to_all | solution.py:335
  40.7 41.1 %all-to-all-start.2 = ((bf16[32,24,1024]{2,1,0:T(8,128)(2,1)}), bf16[32,24,1024]{2,1,0:T(8,128)(2,1)S(1)}, u32[]{:S(2)}, u32[]{:S(2)}) async-start(bf16[32,24,1024]{2,1,0:T(8,128)(2,1)} %shard_map.60), calls=%async_computation.2 | async-start | bytes 3145728 | tf_op jit(solution)/shard_map/all_to_all | solution.py:335
  43.4 38.4 %copy-start = (bf16[1,1024,256]{2,1,0:T(8,128)(2,1)S(1)}, bf16[1,1024,256]{2,1,0:T(8,128)(2,1)}, u32[]{:S(2)}) copy-start(bf16[1,1024,256]{2,1,0:T(8,128)(2,1)} %param.6) | copy-start | bytes 1572868

commit v8 on v7

--- a/solution.py
+++ b/solution.py
@@ -9,7 +9,7 @@
 
 TAYLOR = 4
 RI = 8
-WB = 32
+WB = 16
 BF16 = jnp.bfloat16
 F32 = jnp.float32
 MIB = 1 << 20
@@ -78,9 +78,12 @@
                 in_sems.at[slot],
             )
 
-        def put(group, slot):
+        def put(group, slot, k):
+            at = pl.ds(k * wb, wb)
             return pltpu.make_async_copy(
-                done.at[slot], o_ref.at[:, pl.ds(pl.multiple_of(group * RI, RI), RI), :], out_sems.at[slot]
+                done.at[slot, at],
+                o_ref.at[at, pl.ds(pl.multiple_of(group * RI, RI), RI), :],
+                out_sems.at[slot, k],
             )
 
         if not fresh:
@@ -100,6 +103,13 @@
 
         @pl.loop(0, count)
         def _(group):
+            side = lax.rem(group, 2)
+
+            @pl.when(group >= 2)
+            def _():
+                for k in range(w // wb):
+                    put(group - 2, side, k).wait()
+
             for p in range(pieces):
                 fetch(group, p).wait()
                 later, piece = divmod(p + ahead, pieces)
@@ -108,25 +118,21 @@
                 def _():
                     fetch(group + later, piece).start()
 
-                x = held[lax.rem(group, 2) * pieces + p].reshape(size * RI, n)
+                x = held[side * pieces + p].reshape(size * RI, n)
                 for k in range(w // wb):
                     r = slice(k * wb * RI, (k + 1) * wb * RI)
                     part = jnp.dot(fk_ref[r, p * size * RI : (p + 1) * size * RI], x, preferred_element_type=F32)
                     if p == 0:
                         acc[r] = part
+                    elif p < pieces - 1:
+                        acc[r] += part
                     else:
-                        acc[r] += part
-            slot = lax.rem(group, 2)
-
-            @pl.when(group >= 2)
-            def _():
-                put(group - 2, slot).wait()
-
-            done[slot] = acc[...].reshape(w, RI, n).astype(BF16)
-            put(group, slot).start()
+                        done[side, k * wb : (k + 1) * wb] = (acc[r] + part).reshape(wb, RI, n).astype(BF16)
+                        put(group, side, k).start()
 
         for group in range(max(0, count - 2), count):
-            put(group, group % 2).wait()
+            for k in range(w // wb):
+                put(group, group % 2, k).wait()
         if fresh:
             spread.wait()
 
@@ -143,7 +149,7 @@
             pltpu.VMEM((2, w, RI, n), BF16),
             pltpu.VMEM((w * RI, n), F32),
             pltpu.SemaphoreType.DMA((slots,)),
-            pltpu.SemaphoreType.DMA((2,)),
+            pltpu.SemaphoreType.DMA((2, w // wb)),
             pltpu.SemaphoreType.DMA,
         ],
         cost_estimate=pl.CostEstimate(
@@ -185,7 +191,7 @@
 
 def taylor_kernel(*refs, counts, parts):
     g_refs = refs[: len(counts)]
-    q0_ref, half_ref, new_ref, send_ref, kept_ref, total, even, odd, sems = refs[len(counts) :]
+    q0_ref, half_ref, send_ref, kept_ref, total, even, odd, sems = refs[len(counts) :]
     piece = kept_ref.shape[0] // sems.shape[0]
 
     def keep(i):
@@ -219,7 +225,6 @@
             start += size
         source = target
     fresh = total[...].astype(BF16)
-    new_ref[...] = fresh.reshape(n, cols)
     for b in range(rows // RI):
         send_ref[:, :, b * cols : (b + 1) * cols] = fresh[:, b * RI : (b + 1) * RI]
     pl.loop(0, sems.shape[0])(lambda i: keep(i).wait())
@@ -234,9 +239,8 @@
     return pl.pallas_call(
         functools.partial(taylor_kernel, counts=counts, parts=parts),
         in_specs=[VMEM] * (len(received) + 1) + [HBM],
-        out_specs=[VMEM] * 3,
+        out_specs=[VMEM] * 2,
         out_shape=[
-            jax.ShapeDtypeStruct((n, cols), BF16),
             jax.ShapeDtypeStruct((owners, RI, rows // RI * cols), BF16),
             jax.ShapeDtypeStruct(kept, BF16),
         ],
@@ -253,7 +257,7 @@
 
 
 def bias_kernel(*refs, cols):
-    n_ref, k_ref, h_ref, o_ref, pair, rest, sems = refs
+    n_ref, s_ref, k_ref, h_ref, o_ref, new_ref, pair, rest, sems, new_sems = refs
     w, _, depth = n_ref.shape
     vectors = h_ref.shape[0]
     wb = min(w, WB)
@@ -268,7 +272,15 @@
         at = pl.ds(piece * size, size)
         return pltpu.make_async_copy(h_ref.at[pl.ds(kept + piece * size, size)], rest.at[at], sems.at[piece])
 
+    def put(group):
+        return pltpu.make_async_copy(
+            s_ref.at[:, :, pl.ds(pl.multiple_of(group * cols, cols), cols)],
+            new_ref.at[:, pl.ds(pl.multiple_of(group * RI, RI), RI), :],
+            new_sems.at[group],
+        )
+
     pl.loop(0, (vectors - kept) // size)(lambda piece: fetch(piece).start())
+    pl.loop(0, depth // cols)(lambda group: put(group).start())
 
     def block(k, fetched):
         for s in range(0, depth, cols):
@@ -296,28 +308,33 @@
     block(0, False)
     if w > wb:
         pl.loop(1, w // wb)(lambda k: block(k, True))
-
-
-def bias(rows, kept, halves, cols):
+    pl.loop(0, depth // cols)(lambda group: put(group).wait())
+
+
+def bias(rows, send, kept, halves, cols):
     w, _, depth = rows.shape
     vectors = halves.shape[0]
     wb = min(w, WB)
     return pl.pallas_call(
         functools.partial(bias_kernel, cols=cols),
-        in_specs=[VMEM, VMEM, HBM],
-        out_specs=VMEM,
-        out_shape=jax.ShapeDtypeStruct((w, 2, vectors), F32),
+        in_specs=[VMEM, VMEM, VMEM, HBM],
+        out_specs=[VMEM, HBM],
+        out_shape=[
+            jax.ShapeDtypeStruct((w, 2, vectors), F32),
+            jax.ShapeDtypeStruct((w, depth // cols * RI, cols), BF16),
+        ],
         scratch_shapes=[
             pltpu.VMEM((depth, wb * 2 * RI), BF16),
             pltpu.VMEM((vectors - kept.shape[0],) + halves.shape[1:], BF16),
             pltpu.SemaphoreType.DMA(((vectors - kept.shape[0]) // 128,)),
+            pltpu.SemaphoreType.DMA((depth // cols,)),
         ],
         cost_estimate=pl.CostEstimate(
             flops=2 * vectors * RI * depth * w * 2 * RI, bytes_accessed=vectors * RI * depth * 2, transcendentals=0
         ),
         compiler_params=grant(40),
         name="bias",
-    )(rows, kept, halves)
+    )(rows, send, kept, halves)
 
 
 class Share:
@@ -353,10 +370,11 @@
         received.append(exchange(made, share.axes))
         start += count
     halves = half(trial, chol)
-    fresh, send, kept = taylor(received, counts, share.parts, orbitals[0], halves)
+    send, kept = taylor(received, counts, share.parts, orbitals[0], halves)
     rows_all = exchange(send, "wide")
-    mine = exchange(bias(rows_all, kept, halves, trial.shape[1]), "wide")
-    return fresh[None], mine.sum(axis=0, keepdims=True)
+    partial, fresh = bias(rows_all, send, kept, halves, trial.shape[1])
+    mine = exchange(partial, "wide")
+    return fresh.reshape(orbitals.shape), mine.sum(axis=0, keepdims=True)
 
 
 def solution(mesh):

time: 121 us -> 120 us (level)
  no operation moved by 1% of the time
where the time goes in v8:
time: 120 us
  Pallas kernels  58.9 us (49%)
  blocking collectives  42.2 us (35%)
  waiting for transfers between devices  11.3 us (9%)
  starting transfers between devices  5.31 us (4%)
    all_to_all x3, blocking collectives, exchange(): return lax.all_to_all(v, axes, split_axis=0, concat_axis=0, tiled=True)  42.2 us
    pallas_call x1, Pallas kernels, half(): pl.pallas_call(kernel, grid=(count,), in_specs=[pl.BlockSpec((n, cols), l...  31.7 us
    pallas_call x2, Pallas kernels, gen(): pl.pallas_call(kernel, in_specs=[VMEM if fresh else HBM, HBM], out_specs=...  17.7 us
    all_to_all x2, waiting for transfers between devices, exchange(): return lax.all_to_all(v, axes, split_axis=0, concat_axis=0, tiled=True)  11.3 us
    pallas_call x1, Pallas kernels, bias(): pl.pallas_call(functools.partial(bias_kernel, cols=cols), in_specs=[VMEM,...  6 us
    all_to_all x2, starting transfers between devices, exchange(): return lax.all_to_all(v, axes, split_axis=0, concat_axis=0, tiled=True)  5.31 us
    pallas_call x1, Pallas kernels, taylor(): pl.pallas_call(functools.partial(taylor_kernel, counts=counts, parts=part...  3.47 us
  transfers between devices with their start and end apart: 2, of which 2 were waited for; matrix products, arithmetic and copies ran while one was open for 0% of the time, Pallas kernels for 36%

profile of v8, /device:TPU:0, one launch (start us, length us, event | category | flops | bytes accessed | tf_op | source)
XLA Modules:
  0.0 119.7 jit_solution(4152836693174367938)
XLA Ops:
  0.6 0.0 copy-start.1
  0.6 0.7 copy-done.1
  1.3 14.5 %all_to_all.25.s_ref = bf16[32,4,128]{2,1,0:T(4,128)(2,1)} all-to-all(bf16[32,4,128]{2,1,0:T(4,128)(2,1)S(1)} %copies.1), channel_id=1, replica_groups=mesh['groups'=2,'wide'=16] {'groups','wide'}, dimensions={0} | all-to-all | bytes 65536 | tf_op jit(solution)/shard_map/all_to_all | solution.py:352
  15.8 6.4 %shard_map.59 = (bf16[32,8,1024]{2,1,0:T(8,128)(2,1)}, bf16[256,4096]{1,0:T(8,128)(2,1)}) custom-call(bf16[32,4,128]{2,1,0:T(4,128)(2,1)} %all_to_all.25.s_ref, bf16[512,64,1024]{2,1,0:T(8,128)(2,1)} %x_ref.1), custom_call_target="tpu_custom_call" | custom-call | flops 2147483648 | bytes 8388608 | tf_op jit(solution)/shard_map/pallas_call | solution.py:141
  22.2 2.6 %all-to-all-start.1 = ((bf16[32,8,1024]{2,1,0:T(8,128)(2,1)}), bf16[32,8,1024]{2,1,0:T(8,128)(2,1)S(1)}, u32[]{:S(2)}, u32[]{:S(2)}) async-start(bf16[32,8,1024]{2,1,0:T(8,128)(2,1)} %get-tuple-element.8), calls=%async_computation.1 | async-start | bytes 1048576 | tf_op jit(solution)/shard_map/all_to_all | solution.py:352
  24.9 11.3 %shard_map.60 = bf16[32,24,1024]{2,1,0:T(8,128)(2,1)} custom-call(bf16[256,4096]{1,0:T(8,128)(2,1)} %get-tuple-element.9.s_ref, bf16[512,64,1024]{2,1,0:T(8,128)(2,1)} %x_ref.1), custom_call_target="tpu_custom_call" | custom-call | flops 6442450944 | bytes 25165824 | tf_op jit(solution)/shard_map/pallas_call | solution.py:141
  36.2 4.6 %all-to-all-done.1.refs_0_ = bf16[32,8,1024]{2,1,0:T(8,128)(2,1)S(1)} async-done(((bf16[32,8,1024]{2,1,0:T(8,128)(2,1)}), bf16[32,8,1024]{2,1,0:T(8,128)(2,1)S(1)}, u32[]{:S(2)}, u32[]{:S(2)}) %all-to-all-start.1) | async-done | bytes 524320 | tf_op jit(solution)/shard_map/all_to_all | solution.py:352
  40.8 2.7 %all-to-all-start.2 = ((bf16[32,24,1024]{2,1,0:T(8,128)(2,1)}), bf16[32,24,1024]{2,1,0:T(8,128)(2,1)S(1)}, u32[]{:S(2)}, u32[]{:S(2)}) async-start(bf16[32,24,1024]{2,1,0:T(8,128)(2,1)} %shard_map.60), calls=%async_computation.2 | async-start | bytes 3145728 | tf_op jit(solution)/shard_map/all_to_all | solution.py:352
  43.4 0.0 copy-start
  43.5 31.7 %half.1.refs_3_ = bf16[512,8,2048]{2,1,0:T(8,128)(2,1)} custom-call(bf16[1024,256]{1,0:T(8,128)(2,1)} %t_ref.1, bf16[512,64,1024]{2,1,0:T(8,128)(2,1)} %x_ref.1), custom_call_target="tpu_custom_call" | custom-call | flops 17179869184 | bytes 83886080 | tf_op jit(solution)/shard_map/half/pallas_call | solution.py:173
  75.2 6.7 %all-to-all-done.2.refs_1_ = bf16[32,24,1024]{2,1,0:T(8,128)(2,1)S(1)} async-done(((bf16[32,24,1024]{2,1,0:T(8,128)(2,1)}), bf16[32,24,1024]{2,1,0:T(8,128)(2,1)S(1)}, u32[]{:S(2)}, u32[]{:S(2)}) %all-to-all-start.2) | async-done | bytes 1572896 | tf_op jit(solution)/shard_map/all_to_all | solution.py:352
  81.8 0.0 copy-done
  81.8 3.5 %taylor.1 = (bf16[16,8,2048]{2,1,0:T(8,128)(2,1)S(1)}, bf16[256,8,2048]{2,1,0:T(8,128)(2,1)S(1)}) custom-call(bf16[32,8,1024]{2,1,0:T(8,128)(2,1)S(1)} %all-to-all-done.1.refs_0_, bf16[32,24,1024]{2,1,0:T(8,128)(2,1)S(1)} %all-to-all-done.2.refs_1_, bf16[1024,256]{1,0:T(8,128)(2,1)S(1)} %bitcast.3, bf16[512,8,2048]{2,1,0:T(8,128)(2,1)} %half.1.refs_3_), custom_call_target="tpu_custom_call" | custom-call | flops 2147483648 | bytes 3670016 | tf_op jit(solution)/shard_map/taylor/pallas_call | solution.py:239
  85.3 16.9 %all_to_all.26.refs_0_ = bf16[16,8,2048]{2,1,0:T(8,128)(2,1)S(1)} all-to-all(bf16[16,8,2048]{2,1,0:T(8,128)(2,1)S(1)} %get-tuple-element.10.refs_1_), channel_id=1, replica_groups=mesh['groups'=2,'wide'=16] {'wide'}, dimensions={0} | all-to-all | bytes 1048576 | tf_op jit(solution)/shard_map/all_to_all | solution.py:352
  102.3 6.0 %bias.1 = (f32[16,2,512]{2,1,0:T(2,128)S(1)}, bf16[16,64,256]{2,1,0:T(8,128)(2,1)}) custom-call(bf16[16,8,2048]{2,1,0:T(8,128)(2,1)S(1)} %all_to_all.26.refs_0_, bf16[16,8,2048]{2,1,0:T(8,128)(2,1)S(1)} %get-tuple-element.10.refs_1_, bf16[256,8,2048]{2,1,0:T(8,128)(2,1)S(1)} %get-tuple-element.11.refs_2_, bf16[512,8,2048]{2,1,0:T(8,128)(2,1)} %half.1.refs_3_), custom_call_target="tpu_custom_call" | custom-call | flops 4294967296 | bytes 16777216 | tf_op jit(solution)/shard_map/bias/pallas_call | solution.py:318
  108.3 10.8 %all_to_all.27 = f32[16,2,512]{2,1,0:T(2,128)S(1)} all-to-all(f32[16,2,512]{2,1,0:T(2,128)S(1)} %get-tuple-element.13), channel_id=1, replica_groups=mesh['groups'=2,'wide'=16] {'wide'}, dimensions={0} | all-to-all | bytes 131072 | tf_op jit(solution)/shard_map/all_to_all | solution.py:352
  119.1 0.6 reduce_sum.9
  (1 shorter events, 0.0 us)
Async XLA Ops:
  0.6 0.7 copy-start.1
  22.2 18.5 %all-to-all-start.1 = ((bf16[32,8,1024]{2,1,0:T(8,128)(2,1)}), bf16[32,8,1024]{2,1,0:T(8,128)(2,1)S(1)}, u32[]{:S(2)}, u32[]{:S(2)}) async-start(bf16[32,8,1024]{2,1,0:T(8,128)(2,1)} %get-tuple-element.8), calls=%async_computation.1 | async-start | bytes 1048576 | tf_op jit(solution)/shard_map/all_to_all | solution.py:352
  40.8 41.1 %all-to-all-start.2 = ((bf16[32,24,1024]{2,1,0:T(8,128)(2,1)}), bf16[32,24,1024]{2,1,0:T(8,128)(2,1)S(1)}, u32[]{:S(2)}, u32[]{:S(2)}) async-start(bf16[32,24,1024]{2,1,0:T(8,128)(2,1)} %shard_map.60), calls=%async_computation.2 | async-start | bytes 3145728 | tf_op jit(solution)/shard_map/all_to_all | solution.py:352
  43.4 38.4 %copy-start = (bf16[1,1024,256]{2,1,0:T(8,128)(2,1)S(1)}, bf16[1,1024,256]{2,1,0:T(8,128)(2,1)}, u32[]{:S(2)}) copy-start(bf16[1,1024,256]{2,1,0:T(8,128)(2,1)} %param.6) | copy-start | bytes 1572868
